TPU v7x, 256 devices: a whole 4x4x8 slice. The times are simulated.
256 devices in a mesh: expert: 64 (over y, z, core), fsdp: 4 (over x).
Axes of the slice: x: 4, y: 4, z: 8, core: 2. Of those that a mesh axis runs over, the one named last changes fastest.
Arguments:
- feats: bfloat16 [1024, 128, 1536], P('expert', None, 'fsdp'), may hold values from -6 to 6
- cotan: bfloat16 [1024, 128, 1536], P('expert', None, 'fsdp'), may hold values from -6 to 6
- lang: int32 [1024], P('expert'), may hold values from 0 to 63, as said below
- w_out: bfloat16 [64, 1536, 1536], P('expert', 'fsdp'), may hold values from -0.15625 to 0.15625
- gain: bfloat16 [64, 1536], P('expert', 'fsdp'), may hold values from 0.099609375 to 1.8984375
- kernel: bfloat16 [64, 31, 1536], P('expert', None, 'fsdp'), may hold values from -1 to 1
Outputs:
- feat_grad: bfloat16 [1024, 128, 1536], P('expert', None, 'fsdp')
- w_grad: bfloat16 [64, 1536, 1536], P('expert', 'fsdp')
- gain_grad: float32 [64, 1536], P('expert', 'fsdp')
- kernel_grad: float32 [64, 31, 1536], P('expert', None, 'fsdp')
Inputs may be any that keep to these rules, and one draw needn't show every extreme that they name: `lang`: each index of the expert axis holds either none or exactly 1 segments of a language, and each language has exactly 16 segments in all.
All inputs are finite; a program needn't handle non-finite values.
Results may differ from a plain program's by a relative error of at most 0.005.
Values may be sent and summed in bfloat16 or wider, within the bound.
A program may use at most 128 MiB of HBM per device.

v0:
```python
import jax
import jax.numpy as jnp
from jax import lax
from jax.sharding import PartitionSpec as P


def normalize(values, feature_total):
    value_sum = lax.psum(jnp.sum(values, axis=-1), "fsdp")
    centre = values - (value_sum / feature_total)[..., None]
    square_sum = lax.psum(jnp.sum(centre * centre, axis=-1), "fsdp")
    row_var = square_sum / feature_total
    inv_std = lax.rsqrt(row_var + 1e-05)[..., None]
    return (centre * inv_std, inv_std)


def forward_part(inputs, norm_gain, conv_taps, feature_total):
    normed, inv_std = normalize(inputs.astype(jnp.float32), feature_total)
    scaled = normed * norm_gain
    tap_count = conv_taps.shape[0]
    half_width = tap_count // 2
    frames = inputs.shape[1]
    padded = jnp.pad(scaled, ((0, 0), (half_width, half_width), (0, 0)))
    conv_out = jnp.zeros_like(scaled)
    for offset in range(tap_count):
        conv_out = conv_out + conv_taps[offset] * padded[:, offset : offset + frames]
    gate_sig = jax.nn.sigmoid(conv_out)
    hidden = (conv_out * gate_sig).astype(jnp.bfloat16)
    return (normed, inv_std, padded, conv_out, gate_sig, hidden)


def back_split(
    hid_grad,
    grads_in,
    normed,
    inv_std,
    padded,
    conv_out,
    gate_sig,
    norm_gain,
    conv_taps,
    feature_total,
):
    tap_count = conv_taps.shape[0]
    half_width = tap_count // 2
    frames = normed.shape[1]
    conv_grad = hid_grad * gate_sig * (1.0 + conv_out * (1.0 - gate_sig))
    grad_padded = jnp.pad(conv_grad, ((0, 0), (half_width, half_width), (0, 0)))
    scaled_grad = jnp.zeros_like(conv_grad)
    tap_grads = []
    for offset in range(tap_count):
        first_row = 2 * half_width - offset
        scaled_grad = (
            scaled_grad + conv_taps[offset] * grad_padded[:, first_row : first_row + frames]
        )
        tap_grads.append(jnp.sum(conv_grad * padded[:, offset : offset + frames], axis=(0, 1)))
    gain_grad = jnp.sum(scaled_grad * normed, axis=(0, 1))
    norm_grad = scaled_grad * norm_gain
    grad_total, cross_total = lax.psum(
        (jnp.sum(norm_grad, axis=-1), jnp.sum(norm_grad * normed, axis=-1)), "fsdp"
    )
    branch = inv_std * (
        norm_grad
        - (grad_total / feature_total)[..., None]
        - normed * (cross_total / feature_total)[..., None]
    )
    input_grad = (grads_in.astype(jnp.float32) + branch).astype(jnp.bfloat16)
    return (input_grad, gain_grad, jnp.stack(tap_grads))


def arrival_map(recv_occupied, seg_count):
    flat_occupied = recv_occupied.reshape(-1)
    order_pos = jnp.cumsum(flat_occupied) - 1
    position = jnp.arange(seg_count, dtype=jnp.int32)
    return ((order_pos[None, :] == position[:, None]) & (flat_occupied[None, :] > 0)).astype(
        jnp.bfloat16
    )


def compact_rows(compact_map, received, row_shape):
    flat = received.reshape(compact_map.shape[1], -1)
    return (
        jnp.dot(compact_map, flat, preferred_element_type=jnp.float32)
        .astype(jnp.bfloat16)
        .reshape(row_shape)
    )


def per_device(feats, cotan, lang, w_out, gain, kernel):
    seg_count, frames, part_width = feats.shape
    owners = lax.axis_size("expert")
    feature_total = part_width * lax.axis_size("fsdp")
    capacity = max(1, 2 * seg_count // owners)
    slot_count = owners * capacity
    position = jnp.arange(seg_count, dtype=jnp.int32)
    earlier_same = (lang[:, None] == lang[None, :]) & (position[:, None] < position[None, :])
    slot_rank = jnp.sum(earlier_same.astype(jnp.int32), axis=0)
    slot_of = lang * capacity + slot_rank
    routing = jnp.arange(slot_count, dtype=jnp.int32)[:, None] == slot_of[None, :]
    routing_b = routing.astype(jnp.bfloat16)
    send_x = (
        jnp.dot(routing_b, feats.reshape(seg_count, -1), preferred_element_type=jnp.float32)
        .astype(jnp.bfloat16)
        .reshape(owners, capacity, -1)
    )
    send_dy = (
        jnp.dot(routing_b, cotan.reshape(seg_count, -1), preferred_element_type=jnp.float32)
        .astype(jnp.bfloat16)
        .reshape(owners, capacity, -1)
    )
    occupied = jnp.sum(routing.astype(jnp.int32), axis=1).reshape(owners, capacity)
    norm_gain = gain[0].astype(jnp.float32)
    conv_taps = kernel[0].astype(jnp.float32)
    row_shape = (seg_count, frames, part_width)
    recv_x, recv_dy, recv_occupied = (
        lax.all_to_all(send_x, "expert", split_axis=0, concat_axis=0, tiled=True),
        lax.all_to_all(send_dy, "expert", split_axis=0, concat_axis=0, tiled=True),
        lax.all_to_all(occupied, "expert", split_axis=0, concat_axis=0, tiled=True),
    )
    compact_map = arrival_map(recv_occupied, seg_count)
    own_x = compact_rows(compact_map, recv_x, row_shape)
    forward = forward_part(own_x, norm_gain, conv_taps, feature_total)
    own_dy = compact_rows(compact_map, recv_dy, row_shape)
    normed, inv_std, padded, conv_out, gate_sig, hidden = forward
    grad_scale = float(seg_count * frames) ** (-0.5)
    hidden_rows = hidden.reshape(-1, part_width)
    w_rows = w_out[0]
    shard_part = lax.all_gather(own_dy.reshape(-1, part_width), "fsdp", axis=1, tiled=True)
    hid_sum = jnp.dot(shard_part, w_rows.T, preferred_element_type=jnp.float32)
    w_block = jnp.dot(hidden_rows.T, shard_part, preferred_element_type=jnp.float32) * grad_scale
    w_sum = w_block
    hid_sum, w_sum = (hid_sum, w_sum)
    hid_grad = hid_sum.reshape(row_shape)
    input_grad, gain_grad, tap_grad = back_split(
        hid_grad,
        own_dy,
        normed,
        inv_std,
        padded,
        conv_out,
        gate_sig,
        norm_gain,
        conv_taps,
        feature_total,
    )
    back_slots = jnp.dot(
        compact_map.T, input_grad.reshape(seg_count, -1), preferred_element_type=jnp.float32
    ).astype(jnp.bfloat16)
    home_slots = lax.all_to_all(
        back_slots.reshape(owners, capacity, -1), "expert", split_axis=0, concat_axis=0, tiled=True
    )
    feat_grad = (
        jnp.dot(routing_b.T, home_slots.reshape(slot_count, -1), preferred_element_type=jnp.float32)
        .astype(jnp.bfloat16)
        .reshape(feats.shape)
    )
    return (
        feat_grad,
        w_sum.astype(jnp.bfloat16)[None],
        (gain_grad * grad_scale)[None],
        (tap_grad * grad_scale)[None],
    )


def solution(mesh):
    in_specs = (
        P("expert", None, "fsdp"),
        P("expert", None, "fsdp"),
        P("expert"),
        P("expert", "fsdp", None),
        P("expert", "fsdp"),
        P("expert", None, "fsdp"),
    )
    out_specs = (
        P("expert", None, "fsdp"),
        P("expert", "fsdp", None),
        P("expert", "fsdp"),
        P("expert", None, "fsdp"),
    )
    return jax.shard_map(
        per_device, mesh=mesh, in_specs=in_specs, out_specs=out_specs, check_vma=False
    )
```

profile of v0, /device:TPU:1, one launch (start us, length us, event | category | flops | bytes accessed | tf_op | source)
XLA Modules:
  0.0 767.7 jit_solution(10264356971203967042)
XLA Ops:
  7.2 0.9 convert_reduce_fusion.1
  8.0 0.7 add.216
  8.8 0.7 copy.22
  9.5 13.1 %all-to-all-start = ((s32[64,1,1]{2,1,0:T(1,128)}), s32[64,1,1]{2,1,0:T(1,128)S(1)}, u32[]{:S(2)}, u32[]{:S(2)}) async-start(s32[64,1,1]{2,1,0:T(1,128)} %copy.22), calls=%async_computation | async-start | bytes 65536 | tf_op jit(solution)/shard_map/all_to_all | solution.py:117
  22.6 2.3 copy.30
  25.0 4.6 fusion
  29.5 0.5 broadcast.97
  30.1 9.1 %reduce.68 = bf16[64,49152]{1,0:T(8,128)(2,1)} reduce(bf16[64,1,49152]{2,0,1:T(8,128)(2,1)} %fusion, bf16[]{:T(256)} %broadcast.97), dimensions={1}, to_apply=%copy.24.reduce_sub_computation | reduce | bytes 12582914 | tf_op jit(solution)/shard_map/reshape | solution.py:108
  39.2 9.7 %reshape.696 = bf16[64,2,24576]{2,1,0:T(2,128)(2,1)} reshape(bf16[64,49152]{1,0:T(8,128)(2,1)} %reduce.68) | data formatting | bytes 12582912
  48.8 11.0 %all-to-all-start.1 = ((bf16[64,2,24576]{2,1,0:T(2,128)(2,1)}), bf16[64,2,24576]{2,1,0:T(2,128)(2,1)}, u32[]{:S(2)}, u32[]{:S(2)}) async-start(bf16[64,2,24576]{2,1,0:T(2,128)(2,1)} %reshape.696), calls=%async_computation.1 | async-start | bytes 12582912 | tf_op jit(solution)/shard_map/all_to_all | solution.py:116
  59.9 0.9 copy.32
  60.8 4.5 fusion.1
  65.3 9.1 %reduce.69 = bf16[64,49152]{1,0:T(8,128)(2,1)} reduce(bf16[64,1,49152]{2,0,1:T(8,128)(2,1)} %fusion.1, bf16[]{:T(256)} %broadcast.97), dimensions={1}, to_apply=%copy.25.reduce_sub_computation | reduce | bytes 12582914 | tf_op jit(solution)/shard_map/reshape | solution.py:103
  74.4 9.6 %reshape.698 = bf16[64,2,24576]{2,1,0:T(2,128)(2,1)} reshape(bf16[64,49152]{1,0:T(8,128)(2,1)} %reduce.69) | data formatting | bytes 12582912
  84.0 116.5 %all-to-all-done.1 = bf16[64,2,24576]{2,1,0:T(2,128)(2,1)} async-done(((bf16[64,2,24576]{2,1,0:T(2,128)(2,1)}), bf16[64,2,24576]{2,1,0:T(2,128)(2,1)}, u32[]{:S(2)}, u32[]{:S(2)}) %all-to-all-start.1) | async-done | bytes 6291488 | tf_op jit(solution)/shard_map/all_to_all | solution.py:116
  200.5 6.0 all-to-all-start.2
  207.0 1.2 compare_reduce_fusion
  208.2 36.8 %reshape.697 = bf16[64,1,49152]{2,1,0:T(2,128)(2,1)} reshape(bf16[64,2,24576]{2,1,0:T(2,128)(2,1)} %all-to-all-done.1) | data formatting | bytes 12582912
  245.0 11.3 %convolution_convert_fusion.5 = bf16[16,49152]{1,0:T(8,128)(2,1)S(1)} fusion(bf16[64,1,49152]{2,1,0:T(2,128)(2,1)} %reshape.697, s32[64]{0:T(128)S(1)} %add_reduce_fusion, pred[64]{0:T(512)(128)(4,1)S(1)} %compare_reduce_fusion), kind=kOutput, calls=%fused_computation.9 | convolution fusion | flops 101451776 | bytes 7864640 | tf_op jit(solution)/shard_map/dot_general | solution.py:82
  256.3 1.6 reshape_reshape.3
  258.2 89.1 %all-to-all-done.2 = bf16[64,2,24576]{2,1,0:T(2,128)(2,1)} async-done(((bf16[64,2,24576]{2,1,0:T(2,128)(2,1)}), bf16[64,2,24576]{2,1,0:T(2,128)(2,1)}, u32[]{:S(2)}, u32[]{:S(2)}) %all-to-all-start.2) | async-done | bytes 6291488 | tf_op jit(solution)/shard_map/all_to_all | solution.py:115
  347.3 37.2 %reshape.699 = bf16[64,1,49152]{2,1,0:T(2,128)(2,1)} reshape(bf16[64,2,24576]{2,1,0:T(2,128)(2,1)} %all-to-all-done.2) | data formatting | bytes 12582912
  384.5 11.3 %fusion.3 = f32[16,49152]{1,0:T(8,128)S(1)} fusion(bf16[64,1,49152]{2,1,0:T(2,128)(2,1)} %reshape.699, s32[64]{0:T(128)S(1)} %add_reduce_fusion, pred[64]{0:T(512)(128)(4,1)S(1)} %compare_reduce_fusion), kind=kOutput, calls=%fused_computation.8 | convolution fusion | flops 102238208 | bytes 9437504 | tf_op jit(solution)/shard_map/dot_general | solution.py:82
  395.8 0.6 copy.33
  396.4 2.3 copy.31
  399.3 8.6 %psum.28 = f32[16,128]{1,0:T(8,128)S(1)} all-reduce(f32[16,128]{1,0:T(8,128)S(1)} %bitcast_reduce_fusion), channel_id=1, replica_groups=mesh['expert'=64,'fsdp'=4] {'fsdp'}, use_global_device_ids=true, to_apply=%region_4.5 | all-reduce | flops 2048 | bytes 16384 | tf_op jit(solution)/shard_map/psum | solution.py:8
  407.9 2.5 multiply_reduce_fusion.33
  410.5 6.1 psum.29
  416.6 2.4 fusion.74
  419.0 1.7 copy-done.3
  420.8 13.3 %multiply_convert_fusion = (bf16[16,128,384]{2,1,0:T(8,128)(2,1)S(1)}, f32[16,128,384]{2,1,0:T(8,128)}) fusion(f32[384]{0:T(512)S(1)} %get-tuple-element.39, f32[384]{0:T(512)S(1)} %get-tuple-element.40, f32[384]{0:T(512)S(1)} %get-tuple-element.41, f32[384]{0:T(512)S(1)} %get-tuple-element.42, f32[384]{0:T(512)S(1)} %get-tuple-element.43, ...), kind=kLoop, calls=%fused_computation.172 | loop fusion | flops 51904512 | bytes 7911936 | tf_op jit(solution)/shard_map/convert_element_type | solution.py:27
  434.1 27.7 %multiply_reduce_fusion.18 = (f32[384]{0:T(512)S(1)}, f32[384]{0:T(512)S(1)}, f32[384]{0:T(512)S(1)}, f32[384]{0:T(512)S(1)}, f32[384]{0:T(512)S(1)}, /*index=5*...) fusion(f32[16,128,384]{2,1,0:T(8,128)} %copy-done.3, ...), kind=kOutput, calls=%fused_computation.158 | convolution fusion | flops 2442651136 | bytes 16928256 | tf_op jit(solution)/shard_map/dot_general | solution.py:128
  461.8 53.3 %multiply_reduce_fusion.31 = (f32[384]{0:T(512)S(1)}, f32[16,128]{1,0:T(8,128)S(1)}, f32[16,128]{1,0:T(8,128)S(1)}, f32[16,128,384]{2,1,0:T(8,128)}) fusion(f32[2,8,128,384]{3,2,1,0:T(8,128)} %copy-done.2, f32[16,128]{1,0:T(8,128)S(1)} %add_rsqrt_fusion, f32[16,128]{1,0:T(8,128)S(1)} %broadcast_multiply_fusion.3, f32[384]{0:T(512)S(1)} %convert_reduce_fusion.2, ...), kind=kLoop, calls=%fused_computation.171 | loop fusion | flops 54259328 | bytes 9520640 | tf_op jit(solution)/shard_map/reduce_sum | solution.py:56
  515.1 12.4 %all-reduce.2 = (f32[16,128]{1,0:T(8,128)S(1)}, f32[16,128]{1,0:T(8,128)S(1)}) all-reduce(f32[16,128]{1,0:T(8,128)S(1)} %get-tuple-element.5, f32[16,128]{1,0:T(8,128)S(1)} %get-tuple-element.37), channel_id=1, replica_groups=mesh['expert'=64,'fsdp'=4] {'fsdp'}, use_global_device_ids=true, to_apply=%region_10.11 | all-reduce | flops 4096 | bytes 32768 | tf_op jit(solution)/shard_map/psum | solution.py:58
  527.5 4.4 fusion.70
  531.9 0.9 copy.34
  532.9 4.5 fusion.2
  537.4 9.1 %reduce.70 = bf16[64,49152]{1,0:T(8,128)(2,1)} reduce(bf16[64,1,49152]{2,0,1:T(8,128)(2,1)} %fusion.2, bf16[]{:T(256)} %broadcast.97), dimensions={1}, to_apply=%copy.26.reduce_sub_computation | reduce | bytes 12582914 | tf_op jit(solution)/shard_map/reshape | solution.py:149
  546.5 9.7 %reshape.700 = bf16[64,2,24576]{2,1,0:T(2,128)(2,1)} reshape(bf16[64,49152]{1,0:T(8,128)(2,1)} %reduce.70) | data formatting | bytes 12582912
  556.1 14.1 %all-to-all-start.3 = ((bf16[64,2,24576]{2,1,0:T(2,128)(2,1)}), bf16[64,2,24576]{2,1,0:T(2,128)(2,1)}, u32[]{:S(2)}, u32[]{:S(2)}) async-start(bf16[64,2,24576]{2,1,0:T(2,128)(2,1)} %reshape.700), calls=%async_computation.3 | async-start | bytes 12582912 | tf_op jit(solution)/shard_map/all_to_all | solution.py:148
  570.2 0.6 mul.824
  570.9 29.9 %multiply_reduce_fusion = (f32[384]{0:T(512)S(1)}, f32[384]{0:T(512)S(1)}, f32[384]{0:T(512)S(1)}, f32[384]{0:T(512)S(1)}, f32[384]{0:T(512)S(1)}, /*index=5*/f3...) fusion(f32[16,128,384]{2,1,0:T(8,128)} %get-tuple-element.74, ...), kind=kLoop, calls=%fused_computation.140 | loop fusion | flops 28304640 | bytes 6319104 | tf_op jit(solution)/shard_map/reduce_sum | solution.py:55
  601.1 0.7 broadcast_multiply_fusion
  601.7 6.4 fusion.73
  608.2 102.7 %all-to-all-done.3 = bf16[64,2,24576]{2,1,0:T(2,128)(2,1)} async-done(((bf16[64,2,24576]{2,1,0:T(2,128)(2,1)}), bf16[64,2,24576]{2,1,0:T(2,128)(2,1)}, u32[]{:S(2)}, u32[]{:S(2)}) %all-to-all-start.3) | async-done | bytes 6291488 | tf_op jit(solution)/shard_map/all_to_all | solution.py:148
  710.8 36.8 %reshape.701 = bf16[64,1,49152]{2,1,0:T(2,128)(2,1)} reshape(bf16[64,2,24576]{2,1,0:T(2,128)(2,1)} %all-to-all-done.3) | data formatting | bytes 12582912
  747.6 11.4 %convolution_convert_fusion.3 = bf16[16,49152]{1,0:T(8,128)(2,1)S(1)} fusion(bf16[64,1,49152]{2,1,0:T(2,128)(2,1)} %reshape.701, s32[16]{0:T(128)S(1)} %add.216), kind=kOutput, calls=%fused_computation.6 | convolution fusion | flops 101450752 | bytes 7864384 | tf_op jit(solution)/shard_map/dot_general | solution.py:152
  759.0 1.4 copy.35
  (60 shorter events, 1.8 us)
Async XLA Ops:
  7.2 426.9 %copy-start = (bf16[1,384,1536]{2,1,0:T(8,128)(2,1)S(1)}, bf16[1,384,1536]{2,1,0:T(8,128)(2,1)}, u32[]{:S(2)}) copy-start(bf16[1,384,1536]{2,1,0:T(8,128)(2,1)} %param.9) | copy-start | bytes 3538948
  9.5 39.3 %all-to-all-start = ((s32[64,1,1]{2,1,0:T(1,128)}), s32[64,1,1]{2,1,0:T(1,128)S(1)}, u32[]{:S(2)}, u32[]{:S(2)}) async-start(s32[64,1,1]{2,1,0:T(1,128)} %copy.22), calls=%async_computation | async-start | bytes 65536 | tf_op jit(solution)/shard_map/all_to_all | solution.py:117
  48.8 11.0 %copy-start.4 = (bf16[16,128,384]{2,1,0:T(8,128)(2,1)S(1)}, bf16[16,128,384]{2,1,0:T(8,128)(2,1)}, u32[]{:S(2)}) copy-start(bf16[16,128,384]{2,1,0:T(8,128)(2,1)} %param.6) | copy-start | bytes 4718596
  48.8 151.6 %all-to-all-start.1 = ((bf16[64,2,24576]{2,1,0:T(2,128)(2,1)}), bf16[64,2,24576]{2,1,0:T(2,128)(2,1)}, u32[]{:S(2)}, u32[]{:S(2)}) async-start(bf16[64,2,24576]{2,1,0:T(2,128)(2,1)} %reshape.696), calls=%async_computation.1 | async-start | bytes 12582912 | tf_op jit(solution)/shard_map/all_to_all | solution.py:116
  200.5 146.8 %all-to-all-start.2 = ((bf16[64,2,24576]{2,1,0:T(2,128)(2,1)}), bf16[64,2,24576]{2,1,0:T(2,128)(2,1)}, u32[]{:S(2)}, u32[]{:S(2)}) async-start(bf16[64,2,24576]{2,1,0:T(2,128)(2,1)} %reshape.698), calls=%async_computation.2 | async-start | bytes 12582912 | tf_op jit(solution)/shard_map/all_to_all | solution.py:115
  206.5 227.6 %all-gather.2.cloned.1.call-start = ((), (), s32[]{:S(2)}) async-start(), calls=%async_computation.4 | async-start | bytes 7864320 | tf_op jit(solution)/shard_map/all_gather | solution.py:127
  256.3 1.7 copy-start.5
  256.3 1.7 copy-start.6
  396.4 2.6 copy-start.2
  419.0 1.8 copy-start.3
  556.1 154.7 %all-to-all-start.3 = ((bf16[64,2,24576]{2,1,0:T(2,128)(2,1)}), bf16[64,2,24576]{2,1,0:T(2,128)(2,1)}, u32[]{:S(2)}, u32[]{:S(2)}) async-start(bf16[64,2,24576]{2,1,0:T(2,128)(2,1)} %reshape.700), calls=%async_computation.3 | async-start | bytes 12582912 | tf_op jit(solution)/shard_map/all_to_all | solution.py:148
  747.6 12.8 %copy-start.1 = (bf16[1,384,1536]{2,1,0:T(8,128)(2,1)S(1)}, bf16[1,384,1536]{2,1,0:T(8,128)(2,1)}, u32[]{:S(2)}) copy-start(bf16[1,384,1536]{2,1,0:T(8,128)(2,1)} %param.9) | copy-start | bytes 3538948
Sparse Core Ops, SparseCore 0:
  258.0 68.9 all-gather.1
where the time goes:
time: 780 us; the launch traced here: 768 us
  waiting for transfers between devices  308 us (39%)
  local copies, waits for them, and re-layouts  154 us (20%)
  other arithmetic  137 us (18%)
  matrix products  81.6 us (10%)
  starting transfers between devices  44.5 us (6%)
  blocking collectives  27.1 us (3%)
  between operations  14.8 us (2%)
    unnamed x56, local copies, waits for them, and re-layouts  150 us
    all_to_all x1, waiting for transfers between devices, per_device(): lax.all_to_all(send_dy, 'expert', split_axis=0, concat_axis=0, tiled=True)  116 us
    all_to_all x1, waiting for transfers between devices, per_device(): lax.all_to_all(back_slots.reshape(owners, capacity, -1), 'expert', split_...  103 us
    all_to_all x1, waiting for transfers between devices, per_device(): lax.all_to_all(send_x, 'expert', split_axis=0, concat_axis=0, tiled=True)  89.1 us
    reduce_sum x1, other arithmetic, back_split(): gain_grad = jnp.sum(scaled_grad * normed, axis=(0, 1))  53.3 us
    reduce_sum x1, other arithmetic, back_split(): jnp.sum(conv_grad * padded[:, offset:offset + frames], axis=(0, 1))  29.9 us
    dot_general x1, matrix products, per_device(): hid_sum = jnp.dot(shard_part, w_rows.T, preferred_element_type=jnp.float32)  27.7 us
    dot_general x2, matrix products, compact_rows(): jnp.dot(compact_map, flat, preferred_element_type=jnp.float32)  22.6 us
  transfers between devices with their start and end apart: 5, of which 3 were waited for; matrix products, arithmetic and copies ran while one was open for 27% of the time, Pallas kernels for 0%

commit v1 on v0

v1 whole, which is shorter than its diff:
```python
import functools

import jax
import jax.numpy as jnp
from jax import lax
from jax.experimental import pallas as pl
from jax.experimental.pallas import tpu as pltpu
from jax.sharding import PartitionSpec as P

MESH = pl.DeviceIdType.MESH
F32 = jnp.float32
BF16 = jnp.bfloat16
LANES = 128
STEP = 8


def swap_kernel(v_ref, o_ref):
    o_ref[...] = jnp.swapaxes(v_ref[...].astype(F32), 0, 1).astype(BF16)


def to_frames(values):
    segs, frames, width = values.shape
    block = 16
    return pl.pallas_call(
        swap_kernel,
        out_shape=jax.ShapeDtypeStruct((frames, segs, width), BF16),
        grid=(frames // block,),
        in_specs=[pl.BlockSpec((segs, block, width), lambda i: (0, i, 0))],
        out_specs=pl.BlockSpec((block, segs, width), lambda i: (i, 0, 0)),
        cost_estimate=pl.CostEstimate(flops=values.size, bytes_accessed=4 * values.size, transcendentals=0),
        name="to_frames",
    )(values)


def to_segments(values):
    frames, segs, width = values.shape
    block = 16
    return pl.pallas_call(
        swap_kernel,
        out_shape=jax.ShapeDtypeStruct((segs, frames, width), BF16),
        grid=(frames // block,),
        in_specs=[pl.BlockSpec((block, segs, width), lambda i: (i, 0, 0))],
        out_specs=pl.BlockSpec((segs, block, width), lambda i: (0, i, 0)),
        cost_estimate=pl.CostEstimate(flops=values.size, bytes_accessed=4 * values.size, transcendentals=0),
        name="to_segments",
    )(values)


def permute_kernel(dest_ref, v_ref, o_ref):
    total = dest_ref.shape[1]
    rows = o_ref.shape[0] * o_ref.shape[1]
    first = pl.program_id(1) * rows
    out_row = lax.broadcasted_iota(jnp.int32, (rows, total), 0) + first
    pick = jnp.where(out_row == dest_ref[...], 1.0, 0.0).astype(BF16)
    flat = v_ref[...].reshape(total, v_ref.shape[2])
    moved = jnp.dot(pick, flat, preferred_element_type=F32)
    o_ref[...] = moved.astype(BF16).reshape(o_ref.shape)


def permute(dest, values, segs):
    owners, rows, width = values.shape
    part = 16
    return pl.pallas_call(
        permute_kernel,
        out_shape=jax.ShapeDtypeStruct(values.shape, BF16),
        grid=(rows // segs, owners // part),
        in_specs=[
            pl.BlockSpec((1, owners * segs), lambda j, b: (0, 0)),
            pl.BlockSpec((owners, segs, width), lambda j, b: (0, j, 0)),
        ],
        out_specs=pl.BlockSpec((part, segs, width), lambda j, b: (b, j, 0)),
        cost_estimate=pl.CostEstimate(
            flops=2 * owners * segs * values.size, bytes_accessed=4 * values.size, transcendentals=0
        ),
        name="permute_rows",
    )(dest, values)


def exchange_kernel(n, v_ref, o_ref, send_sem, recv_sem):
    me = lax.axis_index("fsdp")
    barrier = pltpu.get_barrier_semaphore()
    for d in range(1, n):
        pl.semaphore_signal(barrier, inc=1, device_id={"fsdp": lax.rem(me + d, n)}, device_id_type=MESH)
    pl.semaphore_wait(barrier, n - 1)
    copies = []
    for d in range(1, n):
        copy = pltpu.make_async_remote_copy(
            src_ref=v_ref,
            dst_ref=o_ref.at[d],
            send_sem=send_sem.at[d],
            recv_sem=recv_sem.at[d],
            device_id={"fsdp": lax.rem(me + d, n)},
            device_id_type=MESH,
        )
        copy.start()
        copies.append(copy)
    o_ref[0] = v_ref[...]
    for copy in copies:
        copy.wait()


def exchange(values, n, cid):
    return pl.pallas_call(
        functools.partial(exchange_kernel, n),
        out_shape=jax.ShapeDtypeStruct((n,) + values.shape, values.dtype),
        in_specs=[pl.BlockSpec(memory_space=pltpu.VMEM)],
        out_specs=pl.BlockSpec(memory_space=pltpu.VMEM),
        scratch_shapes=[pltpu.SemaphoreType.DMA((n,)), pltpu.SemaphoreType.DMA((n,))],
        compiler_params=pltpu.CompilerParams(collective_id=cid, has_side_effects=True),
        name="exchange_sums",
    )(values)


def diagonal(segs):
    lane = lax.broadcasted_iota(jnp.int32, (1, segs, LANES), 2)
    seg = lax.broadcasted_iota(jnp.int32, (1, segs, LANES), 1)
    return lane == seg, lane == seg + LANES // 2


def to_row(first, second, segs):
    low, high = diagonal(segs)
    spread = jnp.where(low, first, 0.0) + jnp.where(high, second, 0.0)
    return jnp.sum(spread, axis=1)


def to_column(row, segs):
    low, _ = diagonal(segs)
    return jnp.sum(jnp.where(low, row[:, None, :], 0.0), axis=2, keepdims=True)


def moments_kernel(x_ref, o_ref):
    width = x_ref.shape[2]
    segs = x_ref.shape[1]
    x = x_ref[...].astype(F32)
    mean = jnp.sum(x, axis=2, keepdims=True) * (1.0 / width)
    centre = x - mean
    square = jnp.sum(centre * centre, axis=2, keepdims=True)
    o_ref[...] = to_row(mean, square, segs)


def moments(x):
    frames, segs, width = x.shape
    block = 16
    return pl.pallas_call(
        moments_kernel,
        out_shape=jax.ShapeDtypeStruct((frames, LANES), F32),
        grid=(frames // block,),
        in_specs=[pl.BlockSpec((block, segs, width), lambda i: (i, 0, 0))],
        out_specs=pl.BlockSpec((block, LANES), lambda i: (i, 0)),
        name="moments",
    )(x)


def mean_and_scale(parts, width):
    n = parts.shape[0]
    rows = [parts[d] for d in range(n)]
    squares = [pltpu.roll(r, LANES // 2, 1) for r in rows]
    mean = sum(rows) * (1.0 / n)
    spread = sum((r - mean) * (r - mean) for r in rows)
    var = (sum(squares) + width * spread) * (1.0 / (n * width))
    return mean, lax.rsqrt(var + 1e-05)


def forward_kernel(width, parts_ref, x_ref, gain_ref, taps_ref, normed_ref, conv_ref, hidden_ref, mean_c, scale_c, padded, tapb):
    frames, segs, _ = x_ref.shape
    taps = taps_ref.shape[0]
    half = taps // 2

    @pl.when(pl.program_id(0) == 0)
    def _():
        mean, scale = mean_and_scale(parts_ref[...], width)
        mean_c[...] = jnp.broadcast_to(to_column(mean, segs), mean_c.shape)
        scale_c[...] = jnp.broadcast_to(to_column(scale, segs), scale_c.shape)

    edge = jnp.zeros((half, segs, LANES), F32)
    padded[:half] = edge
    padded[half + frames :] = jnp.zeros((padded.shape[0] - half - frames, segs, LANES), F32)
    for k in range(taps):
        tapb[k] = jnp.broadcast_to(taps_ref[k : k + 1, :].astype(F32), (8, LANES))
    gain = gain_ref[...].astype(F32)

    def fill(i, carry):
        t = i * STEP
        normed = (x_ref[pl.ds(t, STEP)].astype(F32) - mean_c[pl.ds(t, STEP)]) * scale_c[pl.ds(t, STEP)]
        normed_ref[pl.ds(t, STEP)] = normed
        padded[pl.ds(t + half, STEP)] = normed * gain[None]
        return carry

    lax.fori_loop(0, frames // STEP, fill, 0)

    def convolve(i, carry):
        t = i * STEP
        for h in range(segs // 8):
            acc = [None] * STEP
            for u in range(STEP + taps - 1):
                v = padded[t + u, h * 8 : h * 8 + 8, :]
                for j in range(STEP):
                    k = u - j
                    if 0 <= k < taps:
                        term = tapb[k] * v
                        acc[j] = term if acc[j] is None else acc[j] + term
            for j in range(STEP):
                conv_ref[t + j, h * 8 : h * 8 + 8, :] = acc[j]
        c = conv_ref[pl.ds(t, STEP)]
        hidden_ref[pl.ds(t, STEP)] = (c / (1.0 + jnp.exp(-c))).astype(BF16)
        return carry

    lax.fori_loop(0, frames // STEP, convolve, 0)


def forward(parts, x, gain, taps):
    frames, segs, width = x.shape
    n_taps = taps.shape[0]
    block = pl.BlockSpec((frames, segs, LANES), lambda i: (0, 0, i))
    return pl.pallas_call(
        functools.partial(forward_kernel, width),
        out_shape=(
            jax.ShapeDtypeStruct(x.shape, F32),
            jax.ShapeDtypeStruct(x.shape, F32),
            jax.ShapeDtypeStruct(x.shape, BF16),
        ),
        grid=(width // LANES,),
        in_specs=[
            pl.BlockSpec(parts.shape, lambda i: (0, 0, 0)),
            block,
            pl.BlockSpec((1, LANES), lambda i: (0, i)),
            pl.BlockSpec((n_taps, LANES), lambda i: (0, i)),
        ],
        out_specs=(block, block, block),
        scratch_shapes=[
            pltpu.VMEM((frames, segs, LANES), F32),
            pltpu.VMEM((frames, segs, LANES), F32),
            pltpu.VMEM((frames + 32, segs, LANES), F32),
            pltpu.VMEM((n_taps, 8, LANES), F32),
        ],
        cost_estimate=pl.CostEstimate(flops=80 * x.size, bytes_accessed=12 * x.size, transcendentals=x.size),
        name="forward",
    )(parts, x, gain, taps)


def hid_kernel(order_ref, d0, d1, d2, d3, w_ref, o_ref):
    width = d0.shape[1]
    total = None
    for j, d in enumerate((d0, d1, d2, d3)):
        cols = pl.ds(pl.multiple_of(order_ref[j] * width, LANES), width)
        term = lax.dot_general(
            d[...], w_ref[:, cols], (((1,), (1,)), ((), ())), preferred_element_type=F32
        )
        total = term if total is None else total + term
    o_ref[...] = total


def hid_grads(order, pieces, w):
    rows, width = pieces[0].shape
    block = 256
    return pl.pallas_call(
        hid_kernel,
        out_shape=jax.ShapeDtypeStruct((rows, w.shape[0]), F32),
        grid_spec=pltpu.PrefetchScalarGridSpec(
            num_scalar_prefetch=1,
            grid=(rows // block,),
            in_specs=[pl.BlockSpec((block, width), lambda i, o: (i, 0))] * 4
            + [pl.BlockSpec(w.shape, lambda i, o: (0, 0))],
            out_specs=pl.BlockSpec((block, w.shape[0]), lambda i, o: (i, 0)),
        ),
        cost_estimate=pl.CostEstimate(flops=2 * rows * w.size, bytes_accessed=8 * rows * width, transcendentals=0),
        name="hid_grads",
    )(order, *pieces, w)


def backward_kernel(scale, hid_ref, conv_ref, normed_ref, gain_ref, taps_ref, sg_ref, kg_ref, gg_ref, row_ref, gpad, spad, tapb, sum_a, sum_b):
    frames, segs, _ = hid_ref.shape
    taps = taps_ref.shape[0]
    half = taps // 2
    step = pl.program_id(0)
    tail = gpad.shape[0] - half - frames
    for pad in (gpad, spad):
        pad[:half] = jnp.zeros((half, segs, LANES), F32)
        pad[half + frames :] = jnp.zeros((tail, segs, LANES), F32)
    for k in range(taps):
        tapb[k] = jnp.broadcast_to(taps_ref[k : k + 1, :].astype(F32), (8, LANES))
    gain = gain_ref[...].astype(F32)

    @pl.when(step == 0)
    def _():
        sum_a[...] = jnp.zeros_like(sum_a)
        sum_b[...] = jnp.zeros_like(sum_b)

    def fill(i, carry):
        t = i * STEP
        c = conv_ref[pl.ds(t, STEP)]
        s = 1.0 / (1.0 + jnp.exp(-c))
        gpad[pl.ds(t + half, STEP)] = hid_ref[pl.ds(t, STEP)] * s * (1.0 + c * (1.0 - s))
        spad[pl.ds(t + half, STEP)] = normed_ref[pl.ds(t, STEP)] * gain[None]
        return carry

    lax.fori_loop(0, frames // STEP, fill, 0)

    def transposed(i, gain_sum):
        t = i * STEP
        for h in range(segs // 8):
            rows = slice(h * 8, h * 8 + 8)
            acc = [None] * STEP
            for u in range(STEP + taps - 1):
                v = gpad[t + u, rows, :]
                for j in range(STEP):
                    k = taps - 1 - (u - j)
                    if 0 <= k < taps:
                        term = tapb[k] * v
                        acc[j] = term if acc[j] is None else acc[j] + term
            for j in range(STEP):
                sg_ref[t + j, rows, :] = acc[j]
                normed = normed_ref[t + j, rows, :]
                cross = acc[j] * normed
                gain_sum = gain_sum + cross
                sum_a[t + j, rows, :] += acc[j] * gain
                sum_b[t + j, rows, :] += cross * gain
        return gain_sum

    gain_sum = lax.fori_loop(0, frames // STEP, transposed, jnp.zeros((8, LANES), F32))
    gg_ref[...] = jnp.sum(gain_sum, axis=0, keepdims=True) * scale

    def tap_sums(i, acc):
        t = i * STEP
        acc = list(acc)
        for h in range(segs // 8):
            rows = slice(h * 8, h * 8 + 8)
            g = [gpad[t + half + j, rows, :] for j in range(STEP)]
            for u in range(STEP + taps - 1):
                v = spad[t + u, rows, :]
                for j in range(STEP):
                    k = u - j
                    if 0 <= k < taps:
                        acc[k] = acc[k] + g[j] * v
        return tuple(acc)

    sums = lax.fori_loop(0, frames // STEP, tap_sums, tuple(jnp.zeros((8, LANES), F32) for _ in range(taps)))
    for k in range(taps):
        kg_ref[k : k + 1, :] = jnp.sum(sums[k], axis=0, keepdims=True) * scale

    @pl.when(step == pl.num_programs(0) - 1)
    def _():
        row_ref[...] = to_row(
            jnp.sum(sum_a[...], axis=2, keepdims=True), jnp.sum(sum_b[...], axis=2, keepdims=True), segs
        )


def backward(hid, conv, normed, gain, taps, scale):
    frames, segs, width = hid.shape
    n_taps = taps.shape[0]
    block = pl.BlockSpec((frames, segs, LANES), lambda i: (0, 0, i))
    row = pl.BlockSpec((1, LANES), lambda i: (0, i))
    tap = pl.BlockSpec((n_taps, LANES), lambda i: (0, i))
    return pl.pallas_call(
        functools.partial(backward_kernel, scale),
        out_shape=(
            jax.ShapeDtypeStruct(hid.shape, F32),
            jax.ShapeDtypeStruct((n_taps, width), F32),
            jax.ShapeDtypeStruct((1, width), F32),
            jax.ShapeDtypeStruct((frames, LANES), F32),
        ),
        grid=(width // LANES,),
        in_specs=[block, block, block, row, tap],
        out_specs=(block, tap, row, pl.BlockSpec((frames, LANES), lambda i: (0, 0))),
        scratch_shapes=[
            pltpu.VMEM((frames + 32, segs, LANES), F32),
            pltpu.VMEM((frames + 32, segs, LANES), F32),
            pltpu.VMEM((n_taps, 8, LANES), F32),
            pltpu.VMEM((frames, segs, LANES), F32),
            pltpu.VMEM((frames, segs, LANES), F32),
        ],
        cost_estimate=pl.CostEstimate(flops=160 * hid.size, bytes_accessed=16 * hid.size, transcendentals=hid.size),
        name="backward",
    )(hid, conv, normed, gain, taps)


def finish_kernel(width, parts_ref, sums_ref, sg_ref, normed_ref, dy_ref, gain_ref, o_ref):
    segs = sg_ref.shape[1]
    n = parts_ref.shape[0]
    _, scale = mean_and_scale(parts_ref[...], width)
    total = sum(sums_ref[d] for d in range(n)) * (1.0 / (n * width))
    scale = to_column(scale, segs)
    plain = to_column(total, segs)
    cross = to_column(pltpu.roll(total, LANES // 2, 1), segs)
    branch = scale * (sg_ref[...] * gain_ref[...].astype(F32)[None] - plain - normed_ref[...] * cross)
    o_ref[...] = (dy_ref[...].astype(F32) + branch).astype(BF16)


def finish(parts, sums, sg, normed, dy, gain):
    frames, segs, width = sg.shape
    n = parts.shape[0]
    block = 16
    rows = pl.BlockSpec((n, block, LANES), lambda i: (0, i, 0))
    spec = pl.BlockSpec((block, segs, width), lambda i: (i, 0, 0))
    return pl.pallas_call(
        functools.partial(finish_kernel, width),
        out_shape=jax.ShapeDtypeStruct(sg.shape, BF16),
        grid=(frames // block,),
        in_specs=[rows, rows, spec, spec, spec, pl.BlockSpec((1, width), lambda i: (0, 0))],
        out_specs=spec,
        name="finish",
    )(parts, sums, sg, normed, dy, gain)


def per_device(feats, cotan, lang, w_out, gain, kernel):
    segs, frames, width = feats.shape
    owners = lax.axis_size("expert")
    shards = lax.axis_size("fsdp")
    per = frames // owners
    me = lax.axis_index("fsdp")
    wire = (owners, per * segs, width)
    grad_scale = float(segs * frames) ** (-0.5)

    def all_to_all(v):
        return lax.all_to_all(v, "expert", split_axis=0, concat_axis=0, tiled=True)

    dy_split = all_to_all(to_frames(cotan).reshape(wire))
    langs = all_to_all(jnp.broadcast_to(lang[None, :], (owners, segs))).reshape(-1)
    x_split = all_to_all(to_frames(feats).reshape(wire))

    count = owners * segs
    index = jnp.arange(count, dtype=jnp.int32)
    earlier = (langs[:, None] == langs[None, :]) & (index[:, None] < index[None, :])
    dest = langs * segs + jnp.sum(earlier.astype(jnp.int32), axis=0)
    source = jnp.sum(jnp.where(dest[:, None] == index[None, :], index[:, None], 0), axis=0)
    dest, source = dest[None, :], source[None, :]

    dy = all_to_all(permute(dest, dy_split, segs))
    x = all_to_all(permute(dest, x_split, segs)).reshape(frames, segs, width)

    up = [(i, (i + 1) % shards) for i in range(shards)]
    down = [(i, (i - 1) % shards) for i in range(shards)]
    rows = dy.reshape(frames * segs, width)
    before = lax.ppermute(rows, "fsdp", up)
    after = lax.ppermute(rows, "fsdp", down)
    half = frames * segs // 2
    across = jnp.concatenate(
        [lax.ppermute(before[:half], "fsdp", up), lax.ppermute(after[half:], "fsdp", down)]
    )
    order = jnp.stack([me, (me + 3) % 4, (me + 1) % 4, (me + 2) % 4]).astype(jnp.int32)

    taps = kernel[0]
    parts = exchange(moments(x), shards, 1)
    normed, conv, hidden = forward(parts, x, gain, taps)
    pieces = (rows, before, after, across)
    hid = hid_grads(order, pieces, w_out[0]).reshape(frames, segs, width)
    scaled_grad, tap_grad, gain_grad, sums = backward(hid, conv, normed, gain, taps, grad_scale)
    sums = exchange(sums, shards, 2)
    grads = finish(parts, sums, scaled_grad, normed, dy.reshape(frames, segs, width), gain)
    back = all_to_all(grads.reshape(wire))
    home = all_to_all(permute(source, back, segs))
    feat_grad = to_segments(home.reshape(frames, segs, width))

    full = jnp.concatenate(pieces, axis=1)
    w_rel = lax.dot_general(
        hidden.reshape(-1, width), full, (((0,), (0,)), ((), ())), preferred_element_type=F32
    )
    w_rel = (w_rel * grad_scale).astype(BF16)
    w_grad = jnp.zeros_like(w_rel)
    for j in range(4):
        w_grad = lax.dynamic_update_slice(w_grad, w_rel[:, j * width : (j + 1) * width], (0, order[j] * width))
    return feat_grad, w_grad[None], gain_grad, tap_grad[None]


def solution(mesh):
    in_specs = (
        P("expert", None, "fsdp"),
        P("expert", None, "fsdp"),
        P("expert"),
        P("expert", "fsdp", None),
        P("expert", "fsdp"),
        P("expert", None, "fsdp"),
    )
    out_specs = (
        P("expert", None, "fsdp"),
        P("expert", "fsdp", None),
        P("expert", "fsdp"),
        P("expert", None, "fsdp"),
    )
    return jax.shard_map(
        per_device, mesh=mesh, in_specs=in_specs, out_specs=out_specs, check_vma=False
    )
```

time: 780 us -> 409 us (0.52); the launches traced: 768 us -> 407 us
  local copies, waits for them, and re-layouts: 154 us -> 11.5 us
  other arithmetic: 137 us -> 3.51 us
  Pallas kernels: 0 us -> 115 us
  waiting for transfers between devices: 308 us -> 206 us
  matrix products: 81.6 us -> 6.35 us
  blocking collectives: 27.1 us -> 0 us
  starting transfers between devices: 44.5 us -> 63.5 us
  between operations: 14.8 us -> 0.88 us
    unnamed x56 -> x26, local copies, waits for them, and re-layouts: 150 us -> 7.9 us
    all_to_all x4 -> x7, waiting for transfers between devices: 308 us -> 172 us  [all_to_all(): return lax.all_to_all(v, 'expert', split_axis=0, concat_axis=0, tiled=True)]
    pallas_call x0 -> x13, Pallas kernels: none -> 115 us  [the longest x1 21.1 us: backward(): pl.pallas_call(functools.partial(backward_kernel, scale), out_shape=(jax....]
    reduce_sum x6 -> x2, other arithmetic: 87 us -> 1.51 us  [the longest x1 1.09 us: per_device(): jnp.sum(jnp.where(dest[:, None] == index[None, :], index[:, None], 0), ax...]
    dot_general x8 -> x1, matrix products: 81.6 us -> 6.35 us  [per_device(): lax.dot_general(hidden.reshape(-1, width), full, (((0,), (0,)), ((), ()))...]
    ppermute x0 -> x4, waiting for transfers between devices: none -> 34 us  [the longest x1 34 us: per_device(): before = lax.ppermute(rows, 'fsdp', up)]
    reshape x3 -> x0, other arithmetic: 27.3 us -> none  [the longest x1 9.11 us: per_device(): back_slots.reshape(owners, capacity, -1)]
    psum x3 -> x0, blocking collectives: 27.1 us -> none  [the longest x1 12.4 us: back_split(): lax.psum((jnp.sum(norm_grad, axis=-1), jnp.sum(norm_grad * normed, axis=-...]
  transfers between devices with their start and end apart: 5 -> 11, of which waited for: 3 -> 7; matrix products, arithmetic and copies ran while one was open for 27% -> 3% of each run, Pallas kernels for 0% -> 13%
where the time goes in v1:
time: 409 us; the launch traced here: 407 us
  waiting for transfers between devices  206 us (50%)
  Pallas kernels  115 us (28%)
  starting transfers between devices  63.5 us (16%)
  local copies, waits for them, and re-layouts  11.5 us (3%)
  matrix products  6.35 us (2%)
    all_to_all x7, waiting for transfers between devices, all_to_all(): return lax.all_to_all(v, 'expert', split_axis=0, concat_axis=0, tiled=True)  172 us
    all_to_all x7, starting transfers between devices, all_to_all(): return lax.all_to_all(v, 'expert', split_axis=0, concat_axis=0, tiled=True)  58.1 us
    ppermute x1, waiting for transfers between devices, per_device(): before = lax.ppermute(rows, 'fsdp', up)  34 us
    pallas_call x1, Pallas kernels, backward(): pl.pallas_call(functools.partial(backward_kernel, scale), out_shape=(jax....  21.1 us
    pallas_call x3, Pallas kernels, permute(): pl.pallas_call(permute_kernel, out_shape=jax.ShapeDtypeStruct(values.shap...  20.1 us
    pallas_call x2, Pallas kernels, exchange(): pl.pallas_call(functools.partial(exchange_kernel, n), out_shape=jax.Shape...  20 us
    pallas_call x1, Pallas kernels, forward(): pl.pallas_call(functools.partial(forward_kernel, width), out_shape=(jax.S...  12 us
    pallas_call x2, Pallas kernels, to_frames(): pl.pallas_call(swap_kernel, out_shape=jax.ShapeDtypeStruct((frames, segs,...  11.5 us
  transfers between devices with their start and end apart: 11, of which 7 were waited for; matrix products, arithmetic and copies ran while one was open for 3% of the time, Pallas kernels for 13%

profile of v1, /device:TPU:1, one launch (start us, length us, event | category | flops | bytes accessed | tf_op | source)
XLA Modules:
  0.0 406.7 jit_solution(7479848411824478891)
XLA Ops:
  0.6 1.3 broadcast_in_dim.40
  1.9 13.1 %all-to-all-start = ((s32[64,1,16]{2,1,0:T(1,128)}), s32[64,1,16]{2,1,0:T(1,128)S(1)}, u32[]{:S(2)}, u32[]{:S(2)}) async-start(s32[64,1,16]{2,1,0:T(1,128)} %broadcast_in_dim.40), calls=%async_computation | async-start | bytes 65536 | tf_op jit(solution)/shard_map/all_to_all | solution.py:415
  15.1 5.8 %to_frames.3 = bf16[128,16,384]{2,1,0:T(8,128)(2,1)} custom-call(bf16[16,128,384]{2,1,0:T(8,128)(2,1)} %v_ref.3), custom_call_target="tpu_custom_call" | custom-call | flops 786432 | bytes 3145728 | tf_op jit(solution)/shard_map/to_frames/pallas_call | solution.py:24
  20.8 3.5 all-to-all-done
  24.3 6.9 %all-to-all-start.3 = ((bf16[64,32,384]{2,1,0:T(8,128)(2,1)}), bf16[64,32,384]{2,1,0:T(8,128)(2,1)S(1)}, u32[]{:S(2)}, u32[]{:S(2)}) async-start(bf16[64,32,384]{2,1,0:T(8,128)(2,1)} %bitcast.45), calls=%async_computation.3 | async-start | bytes 3145728 | tf_op jit(solution)/shard_map/all_to_all | solution.py:415
  31.2 5.8 %to_frames.2 = bf16[128,16,384]{2,1,0:T(8,128)(2,1)} custom-call(bf16[16,128,384]{2,1,0:T(8,128)(2,1)} %v_ref.2), custom_call_target="tpu_custom_call" | custom-call | flops 786432 | bytes 3145728 | tf_op jit(solution)/shard_map/to_frames/pallas_call | solution.py:24
  36.9 34.0 %all-to-all-done.3.v_ref = bf16[64,32,384]{2,1,0:T(8,128)(2,1)S(1)} async-done(((bf16[64,32,384]{2,1,0:T(8,128)(2,1)}), bf16[64,32,384]{2,1,0:T(8,128)(2,1)S(1)}, u32[]{:S(2)}, u32[]{:S(2)}) %all-to-all-start.3) | async-done | bytes 1572896 | tf_op jit(solution)/shard_map/all_to_all | solution.py:415
  70.9 1.2 copy-done.8
  72.1 6.1 %all-to-all-start.1 = ((bf16[64,32,384]{2,1,0:T(8,128)(2,1)}), bf16[64,32,384]{2,1,0:T(8,128)(2,1)S(1)}, u32[]{:S(2)}, u32[]{:S(2)}) async-start(bf16[64,32,384]{2,1,0:T(8,128)(2,1)} %bitcast.44), calls=%async_computation.1 | async-start | bytes 3145728 | tf_op jit(solution)/shard_map/all_to_all | solution.py:415
  78.2 0.5 broadcast.27
  78.7 0.8 multiply_reduce_fusion
  79.7 0.4 convert_reduce_fusion
  80.1 0.6 add.48.dest_ref
  80.7 6.7 %permute_rows.4 = bf16[64,32,384]{2,1,0:T(8,128)(2,1)} custom-call(s32[1,1024]{1,0:T(1,128)} %add.48.dest_ref, bf16[64,32,384]{2,1,0:T(8,128)(2,1)} %copy-done.8), custom_call_target="tpu_custom_call" | custom-call | flops 1610612736 | bytes 3145728 | tf_op jit(solution)/shard_map/permute_rows/pallas_call | solution.py:63
  87.4 30.6 %all-to-all-done.1.v_ref = bf16[64,32,384]{2,1,0:T(8,128)(2,1)S(1)} async-done(((bf16[64,32,384]{2,1,0:T(8,128)(2,1)}), bf16[64,32,384]{2,1,0:T(8,128)(2,1)S(1)}, u32[]{:S(2)}, u32[]{:S(2)}) %all-to-all-start.1) | async-done | bytes 1572896 | tf_op jit(solution)/shard_map/all_to_all | solution.py:415
  118.0 6.1 %all-to-all-start.4 = ((bf16[64,32,384]{2,1,0:T(8,128)(2,1)}), bf16[64,32,384]{2,1,0:T(8,128)(2,1)S(1)}, u32[]{:S(2)}, u32[]{:S(2)}) async-start(bf16[64,32,384]{2,1,0:T(8,128)(2,1)} %permute_rows.4), calls=%async_computation.4 | async-start | bytes 3145728 | tf_op jit(solution)/shard_map/all_to_all | solution.py:415
  124.1 6.7 %permute_rows.3 = bf16[64,32,384]{2,1,0:T(8,128)(2,1)} custom-call(s32[1,1024]{1,0:T(1,128)} %add.48.dest_ref, bf16[64,32,384]{2,1,0:T(8,128)(2,1)} %copy-done.7), custom_call_target="tpu_custom_call" | custom-call | flops 1610612736 | bytes 3145728 | tf_op jit(solution)/shard_map/permute_rows/pallas_call | solution.py:63
  130.8 33.0 %all-to-all-done.4 = bf16[64,32,384]{2,1,0:T(8,128)(2,1)S(1)} async-done(((bf16[64,32,384]{2,1,0:T(8,128)(2,1)}), bf16[64,32,384]{2,1,0:T(8,128)(2,1)S(1)}, u32[]{:S(2)}, u32[]{:S(2)}) %all-to-all-start.4) | async-done | bytes 1572896 | tf_op jit(solution)/shard_map/all_to_all | solution.py:415
  163.8 6.1 %all-to-all-start.2 = ((bf16[64,32,384]{2,1,0:T(8,128)(2,1)}), bf16[64,32,384]{2,1,0:T(8,128)(2,1)S(1)}, u32[]{:S(2)}, u32[]{:S(2)}) async-start(bf16[64,32,384]{2,1,0:T(8,128)(2,1)} %permute_rows.3), calls=%async_computation.2 | async-start | bytes 3145728 | tf_op jit(solution)/shard_map/all_to_all | solution.py:415
  169.9 1.3 collective-permute-start
  171.2 1.5 collective-permute-start.1
  172.7 34.0 %collective-permute-done.d1 = bf16[2048,384]{1,0:T(8,128)(2,1)S(1)} collective-permute-done((bf16[2048,384]{1,0:T(8,128)(2,1)S(1)}, bf16[2048,384]{1,0:T(8,128)(2,1)S(1)}, u32[]{:S(2)}, u32[]{:S(2)}) %collective-permute-start) | collective-permute-done | bytes 1572896 | tf_op jit(solution)/shard_map/ppermute | solution.py:434
  206.7 1.1 slice.24
  207.9 0.2 copy-done.4
  208.1 2.7 collective-permute-start.3
  210.8 0.6 pad_add_fusion.order_ref
  211.4 1.1 copy-done
  212.6 5.8 %moments.1.v_ref = f32[128,128]{1,0:T(8,128)} custom-call(bf16[128,16,384]{2,1,0:T(8,128)(2,1)} %bitcast.35), custom_call_target="tpu_custom_call" | custom-call | tf_op jit(solution)/shard_map/moments/pallas_call | solution.py:144
  218.4 11.7 %exchange_sums.2.parts_ref = f32[4,128,128]{2,1,0:T(8,128)} custom-call(f32[128,128]{1,0:T(8,128)} %moments.1.v_ref), custom_call_target="tpu_custom_call" | custom-call | tf_op jit(solution)/shard_map/exchange_sums/pallas_call | solution.py:103
  230.1 12.0 %forward.1 = (f32[128,16,384]{2,1,0:T(8,128)}, f32[128,16,384]{2,1,0:T(8,128)}, bf16[128,16,384]{2,1,0:T(8,128)(2,1)}) custom-call(f32[4,128,128]{2,1,0:T(8,128)} %exchange_sums.2.parts_ref, bf16[128,16,384]{2,1,0:T(8,128)(2,1)} %bitcast.36, bf16[1,384]{1,0:T(2,128)(2,1)} %gain_ref.5, bf16[31,384]{1,0:T(8,128)(2,1)} %bitcast.48), custom_call_target="tpu_custom_call" | custom-call | flops 62914560 | bytes 9437184 | tf_op jit(solution)/shard_map/forward/pallas_call | solution.py:215
  242.1 1.2 constant_dynamic-update-slice_fusion.1
  243.3 0.2 constant_dynamic-update-slice_fusion.d3
  243.5 1.1 copy-done.6
  244.6 10.6 %hid_grads.1 = f32[2048,384]{1,0:T(8,128)} custom-call(s32[4]{0:T(128)} %pad_add_fusion.order_ref, bf16[2048,384]{1,0:T(8,128)(2,1)} %bitcast.39, bf16[2048,384]{1,0:T(8,128)(2,1)} %copy-done.4, bf16[2048,384]{1,0:T(8,128)(2,1)} %copy-done.5, bf16[2048,384]{1,0:T(8,128)(2,1)} %copy-done.6, bf16[384,1536]{1,0:T(8,128)(2,1)} %bitcast.47), custom_call_target="tpu_custom_call" | custom-call | flops 2415919104 | bytes 6291456 | tf_op jit(solution)/shard_map/hid_grads/pallas_call | solution.py:256
  255.3 21.1 %backward.1 = (f32[128,16,384]{2,1,0:T(8,128)}, f32[31,384]{1,0:T(8,128)}, f32[1,384]{1,0:T(1,128)}, f32[128,128]{1,0:T(8,128)}) custom-call(f32[128,16,384]{2,1,0:T(8,128)} %bitcast.42, f32[128,16,384]{2,1,0:T(8,128)} %get-tuple-element.11.conv_ref, f32[128,16,384]{2,1,0:T(8,128)} %get-tuple-element.12.normed_ref, bf16[1,384]{1,0:T(2,128)(2,1)} %gain_ref.5, ...), custom_call_target="tpu_custom_call" | custom-call | flops 125829120 | bytes 12582912 | tf_op jit(solution)/shard_map/backward/pallas_call | solution.py:354
  276.3 8.4 %exchange_sums.3.sums_ref = f32[4,128,128]{2,1,0:T(8,128)} custom-call(f32[128,128]{1,0:T(8,128)} %get-tuple-element.13.v_ref), custom_call_target="tpu_custom_call" | custom-call | tf_op jit(solution)/shard_map/exchange_sums/pallas_call | solution.py:103
  284.7 7.8 %finish.1 = bf16[128,16,384]{2,1,0:T(8,128)(2,1)} custom-call(f32[4,128,128]{2,1,0:T(8,128)} %exchange_sums.2.parts_ref, f32[4,128,128]{2,1,0:T(8,128)} %exchange_sums.3.sums_ref, f32[128,16,384]{2,1,0:T(8,128)} %get-tuple-element.14.sg_ref, f32[128,16,384]{2,1,0:T(8,128)} %get-tuple-element.12.normed_ref, bf16[128,16,384]{2,1,0:T(8,128)(2,1)} %bitcast.40, ...), custom_call_target="tpu_custom_call" | custom-call | tf_op jit(solution)/shard_map/finish/pallas_call | solution.py:395
  292.6 13.6 %all-to-all-start.5 = ((bf16[64,32,384]{2,1,0:T(8,128)(2,1)}), bf16[64,32,384]{2,1,0:T(8,128)(2,1)S(1)}, u32[]{:S(2)}, u32[]{:S(2)}) async-start(bf16[64,32,384]{2,1,0:T(8,128)(2,1)} %bitcast.46), calls=%async_computation.5 | async-start | bytes 3145728 | tf_op jit(solution)/shard_map/all_to_all | solution.py:415
  306.2 1.1 select_reduce_fusion
  307.3 38.7 %all-to-all-done.5.v_ref = bf16[64,32,384]{2,1,0:T(8,128)(2,1)S(1)} async-done(((bf16[64,32,384]{2,1,0:T(8,128)(2,1)}), bf16[64,32,384]{2,1,0:T(8,128)(2,1)S(1)}, u32[]{:S(2)}, u32[]{:S(2)}) %all-to-all-start.5) | async-done | bytes 1572896 | tf_op jit(solution)/shard_map/all_to_all | solution.py:415
  345.9 1.1 copy-done.9
  347.1 6.7 %permute_rows.5 = bf16[64,32,384]{2,1,0:T(8,128)(2,1)} custom-call(s32[1,1024]{1,0:T(1,128)} %bitcast.53, bf16[64,32,384]{2,1,0:T(8,128)(2,1)} %copy-done.9), custom_call_target="tpu_custom_call" | custom-call | flops 1610612736 | bytes 3145728 | tf_op jit(solution)/shard_map/permute_rows/pallas_call | solution.py:63
  353.7 6.2 %all-to-all-start.6 = ((bf16[64,32,384]{2,1,0:T(8,128)(2,1)}), bf16[64,32,384]{2,1,0:T(8,128)(2,1)S(1)}, u32[]{:S(2)}, u32[]{:S(2)}) async-start(bf16[64,32,384]{2,1,0:T(8,128)(2,1)} %permute_rows.5), calls=%async_computation.6 | async-start | bytes 3145728 | tf_op jit(solution)/shard_map/all_to_all | solution.py:415
  360.0 0.7 copy.13
  360.7 6.4 %fusion.12 = bf16[384,1536]{1,0:T(8,128)(2,1)S(1)} fusion(bf16[2048,384]{1,0:T(8,128)(2,1)} %bitcast.52, bf16[2048,384]{1,0:T(8,128)(2,1)} %copy-done.6, bf16[2048,384]{1,0:T(8,128)(2,1)} %copy-done.5, bf16[2048,384]{1,0:T(8,128)(2,1)} %copy-done.4, bf16[2048,384]{1,0:T(8,128)(2,1)S(1)} %bitcast.41), kind=kOutput, calls=%fused_computation.14 | convolution fusion | flops 2442264576 | bytes 9043968 | tf_op jit(solution)/shard_map/dot_general | solution.py:455
  367.4 32.3 %all-to-all-done.6 = bf16[64,32,384]{2,1,0:T(8,128)(2,1)S(1)} async-done(((bf16[64,32,384]{2,1,0:T(8,128)(2,1)}), bf16[64,32,384]{2,1,0:T(8,128)(2,1)S(1)}, u32[]{:S(2)}, u32[]{:S(2)}) %all-to-all-start.6) | async-done | bytes 1572896 | tf_op jit(solution)/shard_map/all_to_all | solution.py:415
  399.7 1.2 copy-done.3
  400.9 5.7 %to_segments.1 = bf16[16,128,384]{2,1,0:T(8,128)(2,1)} custom-call(bf16[128,16,384]{2,1,0:T(8,128)(2,1)} %bitcast.43), custom_call_target="tpu_custom_call" | custom-call | flops 786432 | bytes 3145728 | tf_op jit(solution)/shard_map/to_segments/pallas_call | solution.py:38
  (32 shorter events, 0.6 us)
Async XLA Ops:
  1.9 22.4 %all-to-all-start = ((s32[64,1,16]{2,1,0:T(1,128)}), s32[64,1,16]{2,1,0:T(1,128)S(1)}, u32[]{:S(2)}, u32[]{:S(2)}) async-start(s32[64,1,16]{2,1,0:T(1,128)} %broadcast_in_dim.40), calls=%async_computation | async-start | bytes 65536 | tf_op jit(solution)/shard_map/all_to_all | solution.py:415
  24.3 46.6 %all-to-all-start.3 = ((bf16[64,32,384]{2,1,0:T(8,128)(2,1)}), bf16[64,32,384]{2,1,0:T(8,128)(2,1)S(1)}, u32[]{:S(2)}, u32[]{:S(2)}) async-start(bf16[64,32,384]{2,1,0:T(8,128)(2,1)} %bitcast.45), calls=%async_computation.3 | async-start | bytes 3145728 | tf_op jit(solution)/shard_map/all_to_all | solution.py:415
  70.9 1.2 copy-start.8
  72.1 45.9 %all-to-all-start.1 = ((bf16[64,32,384]{2,1,0:T(8,128)(2,1)}), bf16[64,32,384]{2,1,0:T(8,128)(2,1)S(1)}, u32[]{:S(2)}, u32[]{:S(2)}) async-start(bf16[64,32,384]{2,1,0:T(8,128)(2,1)} %bitcast.44), calls=%async_computation.1 | async-start | bytes 3145728 | tf_op jit(solution)/shard_map/all_to_all | solution.py:415
  118.0 6.1 %copy-start.7 = (bf16[64,32,384]{2,1,0:T(8,128)(2,1)}, bf16[64,32,384]{2,1,0:T(8,128)(2,1)S(1)}, u32[]{:S(2)}) copy-start(bf16[64,32,384]{2,1,0:T(8,128)(2,1)S(1)} %all-to-all-done.1.v_ref) | copy-start | bytes 4718596
  118.0 45.9 %all-to-all-start.4 = ((bf16[64,32,384]{2,1,0:T(8,128)(2,1)}), bf16[64,32,384]{2,1,0:T(8,128)(2,1)S(1)}, u32[]{:S(2)}, u32[]{:S(2)}) async-start(bf16[64,32,384]{2,1,0:T(8,128)(2,1)} %permute_rows.4), calls=%async_computation.4 | async-start | bytes 3145728 | tf_op jit(solution)/shard_map/all_to_all | solution.py:415
  163.8 7.4 %copy-start.1 = (bf16[64,32,384]{2,1,0:T(8,128)(2,1)}, bf16[64,32,384]{2,1,0:T(8,128)(2,1)S(1)}, u32[]{:S(2)}) copy-start(bf16[64,32,384]{2,1,0:T(8,128)(2,1)S(1)} %all-to-all-done.4) | copy-start | bytes 4718596
  163.8 47.6 %all-to-all-start.2 = ((bf16[64,32,384]{2,1,0:T(8,128)(2,1)}), bf16[64,32,384]{2,1,0:T(8,128)(2,1)S(1)}, u32[]{:S(2)}, u32[]{:S(2)}) async-start(bf16[64,32,384]{2,1,0:T(8,128)(2,1)} %permute_rows.3), calls=%async_computation.2 | async-start | bytes 3145728 | tf_op jit(solution)/shard_map/all_to_all | solution.py:415
  169.9 36.8 %collective-permute-start = (bf16[2048,384]{1,0:T(8,128)(2,1)S(1)}, bf16[2048,384]{1,0:T(8,128)(2,1)S(1)}, u32[]{:S(2)}, u32[]{:S(2)}) collective-permute-start(bf16[2048,384]{1,0:T(8,128)(2,1)S(1)} %bitcast.37), channel_id=1, source_target_pairs={{0,1},{1,2},{2,3},{3,0},{4,5},{5,6},{6,7},{7,4},{8,9},{9,10},{10,1... | collective-permute-start | bytes 4718600 | tf_op jit(solution)/shard_map/ppermute | solution.py:434
  171.2 36.6 %collective-permute-start.1 = (bf16[2048,384]{1,0:T(8,128)(2,1)S(1)}, bf16[2048,384]{1,0:T(8,128)(2,1)S(1)}, u32[]{:S(2)}, u32[]{:S(2)}) collective-permute-start(bf16[2048,384]{1,0:T(8,128)(2,1)S(1)} %bitcast.38), channel_id=1, source_target_pairs={{0,3},{1,0},{2,1},{3,2},{4,7},{5,4},{6,5},{7,6},{8,11},{9,8},{10,9... | collective-permute-start | bytes 4718600 | tf_op jit(solution)/shard_map/ppermute | solution.py:435
  206.7 1.4 copy-start.4
  207.8 34.3 %collective-permute-start.2 = (bf16[1024,384]{1,0:T(8,128)(2,1)}, bf16[1024,384]{1,0:T(8,128)(2,1)}, u32[]{:S(2)}, u32[]{:S(2)}) collective-permute-start(bf16[1024,384]{1,0:T(8,128)(2,1)} %slice.24), channel_id=1, source_target_pairs={{0,1},{1,2},{2,3},{3,0},{4,5},{5,6},{6,7},{7,4},{8,9},{9,10},{10,1... | collective-permute-start | bytes 2359304 | tf_op jit(solution)/shard_map/ppermute | solution.py:438
  207.8 3.0 copy-start.5
  208.1 35.2 %collective-permute-start.3 = (bf16[1024,384]{1,0:T(8,128)(2,1)S(1)}, bf16[1024,384]{1,0:T(8,128)(2,1)S(1)}, u32[]{:S(2)}, u32[]{:S(2)}) collective-permute-start(bf16[1024,384]{1,0:T(8,128)(2,1)S(1)} %slice.25), channel_id=1, source_target_pairs={{0,3},{1,0},{2,1},{3,2},{4,7},{5,4},{6,5},{7,6},{8,11},{9,8},{10,9... | collective-permute-start | bytes 2359304 | tf_op jit(solution)/shard_map/ppermute | solution.py:438
  211.4 1.1 copy-start
  243.5 1.1 copy-start.6
  292.6 53.4 %all-to-all-start.5 = ((bf16[64,32,384]{2,1,0:T(8,128)(2,1)}), bf16[64,32,384]{2,1,0:T(8,128)(2,1)S(1)}, u32[]{:S(2)}, u32[]{:S(2)}) async-start(bf16[64,32,384]{2,1,0:T(8,128)(2,1)} %bitcast.46), calls=%async_computation.5 | async-start | bytes 3145728 | tf_op jit(solution)/shard_map/all_to_all | solution.py:415
  345.9 1.1 copy-start.9
  353.7 6.3 %copy-start.11 = (f32[31,384]{1,0:T(8,128)S(1)}, f32[31,384]{1,0:T(8,128)}, u32[]{:S(2)}) copy-start(f32[31,384]{1,0:T(8,128)} %get-tuple-element.17) | copy-start | bytes 142852
  353.7 6.9 %copy-start.2 = (bf16[64,32,384]{2,1,0:T(8,128)(2,1)S(1)}, bf16[64,32,384]{2,1,0:T(8,128)(2,1)}, u32[]{:S(2)}) copy-start(bf16[64,32,384]{2,1,0:T(8,128)(2,1)} %copy-done.1) | copy-start | bytes 4718596
  353.7 46.0 %all-to-all-start.6 = ((bf16[64,32,384]{2,1,0:T(8,128)(2,1)}), bf16[64,32,384]{2,1,0:T(8,128)(2,1)S(1)}, u32[]{:S(2)}, u32[]{:S(2)}) async-start(bf16[64,32,384]{2,1,0:T(8,128)(2,1)} %permute_rows.5), calls=%async_computation.6 | async-start | bytes 3145728 | tf_op jit(solution)/shard_map/all_to_all | solution.py:415
  367.4 39.3 %copy-start.10 = (bf16[1,384,1536]{2,1,0:T(8,128)(2,1)}, bf16[1,384,1536]{2,1,0:T(8,128)(2,1)S(1)}, u32[]{:S(2)}) copy-start(bf16[1,384,1536]{2,1,0:T(8,128)(2,1)S(1)} %fusion.15) | copy-start | bytes 3538948
  399.7 1.2 copy-start.3

commit v2 on v0

v2 whole, which is shorter than its diff:
```python
import functools

import jax
import jax.numpy as jnp
from jax import lax
from jax.experimental import pallas as pl
from jax.experimental.pallas import tpu as pltpu
from jax.sharding import PartitionSpec as P

MESH = pl.DeviceIdType.MESH
F32 = jnp.float32
BF16 = jnp.bfloat16
LANES = 128
STEP = 8
FB = 16


def diagonal(segs):
    lane = lax.broadcasted_iota(jnp.int32, (1, segs, LANES), 2)
    seg = lax.broadcasted_iota(jnp.int32, (1, segs, LANES), 1)
    return lane == seg, lane == seg + LANES // 2


def to_row(first, second, segs):
    low, high = diagonal(segs)
    spread = jnp.where(low, first, 0.0) + jnp.where(high, second, 0.0)
    return jnp.sum(spread, axis=1)


def to_column(row, segs):
    low, _ = diagonal(segs)
    return jnp.sum(jnp.where(low, row[:, None, :], 0.0), axis=2, keepdims=True)


def mean_and_scale(rows, width):
    n = len(rows)
    squares = [pltpu.roll(r, LANES // 2, 1) for r in rows]
    mean = sum(rows) * (1.0 / n)
    spread = sum((r - mean) * (r - mean) for r in rows)
    var = (sum(squares) + width * spread) * (1.0 / (n * width))
    return mean, lax.rsqrt(var + 1e-05)


def module_kernel(
    owners, shards, grad_scale,
    lang_ref, x_ref, dy_ref, w_ref, gain_ref, taps_ref,
    feat_ref, wgrad_ref, ggrad_ref, kgrad_ref,
    langs, s0, s1, r0, r1, dy_own, x_own, ring, pick, pick_t,
    normed, conv, hidden, hid, gpad, spad, tapb, kacc, sum_a, sum_b, scale_c, mom, parts, sums,
    send, recv, ring_send, ring_recv, ex_send, ex_recv,
):
    segs, frames, width = x_ref.shape
    taps = taps_ref.shape[0]
    half = taps // 2
    total = owners * segs
    chunks = width // LANES
    me = lax.axis_index("expert")
    fs = lax.axis_index("fsdp")
    peer_x = [lax.rem(fs + d, shards) for d in range(shards)]

    barrier = pltpu.get_barrier_semaphore()

    def greet(d, carry):
        pl.semaphore_signal(
            barrier, inc=1, device_id={"expert": lax.rem(me + d, owners)}, device_id_type=MESH
        )
        return carry

    lax.fori_loop(1, owners, greet, 0)
    for d in range(1, shards):
        pl.semaphore_signal(barrier, inc=1, device_id={"fsdp": peer_x[d]}, device_id_type=MESH)

    def split_frames(src, dst):
        def block(b, carry):
            rows = src[:, pl.ds(pl.multiple_of(b * FB, FB), FB), :].astype(F32)
            moved = jnp.swapaxes(rows, 0, 1).astype(BF16)
            dst[pl.ds(b * (FB // 2), FB // 2)] = moved.reshape(FB // 2, 2, segs, width)
            return carry

        lax.fori_loop(0, frames // FB, block, 0)

    def scatter(src, dst, i):
        def one(p):
            pltpu.make_async_remote_copy(
                src_ref=src.at[p], dst_ref=dst.at[me], send_sem=send.at[i], recv_sem=recv.at[i],
                device_id={"expert": p}, device_id_type=MESH,
            ).start()

        def both(d, carry):
            one(lax.rem(me + d, owners))
            one(lax.rem(me + owners - d, owners))
            return carry

        lax.fori_loop(1, owners // 2, both, 0)
        one(lax.rem(me + owners // 2, owners))
        pltpu.make_async_copy(src.at[me], dst.at[me], recv.at[i]).start()

    def arrived(src, dst, i):
        pltpu.make_async_copy(src, dst, recv.at[i]).wait()

    def sent(src, dst, i):
        most = pl.ds(0, owners - 1)
        pltpu.make_async_remote_copy(
            src_ref=src.at[most], dst_ref=dst.at[most], send_sem=send.at[i], recv_sem=recv.at[i],
            device_id={"expert": lax.rem(me + 1, owners)}, device_id_type=MESH,
        ).wait_send()

    split_frames(dy_ref, s0)
    langs_own = langs.at[0]
    langs_all = langs.at[1]

    def spread_langs(d, carry):
        langs_own[d] = lang_ref[...]
        return carry

    lax.fori_loop(0, owners, spread_langs, 0)
    pl.semaphore_wait(barrier, owners - 1 + shards - 1)
    scatter(langs_own, langs_all, 0)
    scatter(s0, r0, 1)
    split_frames(x_ref, s1)
    scatter(s1, r1, 2)

    for k in range(taps):
        tapb[k] = jnp.broadcast_to(taps_ref[k : k + 1, :].astype(F32), (segs, width))
    for pad in (gpad, spad):
        pad[:half] = jnp.zeros((half, segs, LANES), F32)
        pad[half + frames :] = jnp.zeros((pad.shape[0] - half - frames, segs, LANES), F32)

    arrived(langs_own, langs_all, 0)
    owner_of = lax.broadcasted_iota(jnp.int32, (owners, LANES), 0).astype(F32)
    before = lax.broadcasted_iota(jnp.int32, (LANES, LANES), 0) < lax.broadcasted_iota(
        jnp.int32, (LANES, LANES), 1
    )
    before = jnp.where(before, 1.0, 0.0).astype(BF16)
    place = lax.broadcasted_iota(jnp.int32, (total, LANES), 0).astype(F32)
    base = jnp.zeros((owners, 1), F32)
    group = LANES // segs
    for q in range(total // LANES):
        row = jnp.sum(langs_all[q * group : (q + 1) * group], axis=0)
        match = jnp.where(owner_of == row, 1.0, 0.0)
        rank = jnp.dot(match.astype(BF16), before, preferred_element_type=F32) + base
        base = base + jnp.sum(match, axis=1, keepdims=True)
        dest = jnp.sum(match * (owner_of * segs + rank), axis=0, keepdims=True)
        pick[:, q * LANES : (q + 1) * LANES] = jnp.where(place == dest, 1.0, 0.0).astype(BF16)
    number = lax.broadcasted_iota(jnp.int32, (16, total), 1)
    which = lax.broadcasted_iota(jnp.int32, (16, total), 0)
    digits = jnp.where(which == 0, number // 32, number % 32).astype(F32).astype(BF16)
    found = lax.dot_general(digits, pick[...], (((1,), (1,)), ((), ())), preferred_element_type=F32)
    source = found[0:1] * 32.0 + found[1:2]
    for q in range(total // LANES):
        cols = slice(q * LANES, (q + 1) * LANES)
        pick_t[:, cols] = jnp.where(place == source[:, cols], 1.0, 0.0).astype(BF16)

    def permute(chosen, src, dst):
        rows = 256

        def block(b, carry):
            choice = chosen[pl.ds(pl.multiple_of(b * rows, rows), rows), :]
            for j in range(2):
                flat = src[:, j].reshape(total, width)
                moved = jnp.dot(choice, flat, preferred_element_type=F32).astype(BF16)
                dst[pl.ds(b * (rows // segs), rows // segs), j] = moved.reshape(rows // segs, segs, width)
            return carry

        lax.fori_loop(0, total // rows, block, 0)

    arrived(s0, r0, 1)
    sent(s0, r0, 1)
    permute(pick, r0, s0)
    scatter(s0, dy_own, 3)
    arrived(s1, r1, 2)
    sent(s1, r1, 2)
    permute(pick, r1, s1)
    scatter(s1, x_own, 4)

    def ring_copy(src, dst, i, d):
        return pltpu.make_async_remote_copy(
            src_ref=src, dst_ref=dst, send_sem=ring_send.at[i], recv_sem=ring_recv.at[i],
            device_id={"fsdp": peer_x[d]}, device_id_type=MESH,
        )

    arrived(s0, dy_own, 3)
    up = ring_copy(dy_own, ring.at[0], 0, 1)
    down = ring_copy(dy_own, ring.at[1], 1, shards - 1)
    up.start()
    down.start()

    def exchange(src, dst, i):
        copies = [
            pltpu.make_async_remote_copy(
                src_ref=src, dst_ref=dst.at[d], send_sem=ex_send.at[i, d], recv_sem=ex_recv.at[i, d],
                device_id={"fsdp": peer_x[d]}, device_id_type=MESH,
            )
            for d in range(1, shards)
        ]
        for copy in copies:
            copy.start()
        return copies

    arrived(s1, x_own, 4)

    def moments(b, carry):
        x = x_own[pl.ds(b * (FB // 2), FB // 2)].astype(F32).reshape(FB, segs, width)
        mean = jnp.sum(x, axis=2, keepdims=True) * (1.0 / width)
        centre = x - mean
        square = jnp.sum(centre * centre, axis=2, keepdims=True)
        mom[0, pl.ds(pl.multiple_of(b * FB, FB), FB)] = to_row(mean, square, segs)
        return carry

    lax.fori_loop(0, frames // FB, moments, 0)
    copies = exchange(mom.at[0], parts, 0)
    up.wait_recv()
    down.wait_recv()
    middle = owners // 2
    up2 = ring_copy(ring.at[0, pl.ds(0, middle)], ring.at[2, pl.ds(0, middle)], 2, 1)
    down2 = ring_copy(ring.at[1, pl.ds(middle, middle)], ring.at[2, pl.ds(middle, middle)], 3, shards - 1)
    up2.start()
    down2.start()
    for copy in copies:
        copy.wait()

    def normalize(b, carry):
        at = pl.ds(pl.multiple_of(b * FB, FB), FB)
        rows = [mom[0, at]] + [parts[d, at] for d in range(1, shards)]
        mean, scale = mean_and_scale(rows, width)
        mean = to_column(mean, segs)
        scale = to_column(scale, segs)
        x = x_own[pl.ds(b * (FB // 2), FB // 2)].astype(F32).reshape(FB, segs, width)
        normed[at] = (x - mean) * scale
        scale_c[at] = jnp.broadcast_to(scale, (FB, segs, LANES))
        return carry

    lax.fori_loop(0, frames // FB, normalize, 0)

    def convolve(lb, carry):
        lanes = pl.ds(pl.multiple_of(lb * LANES, LANES), LANES)
        gain = gain_ref[:, lanes].astype(F32)

        def fill(i, c):
            at = pl.ds(i * FB, FB)
            spad[pl.ds(i * FB + half, FB)] = normed[at, :, lanes] * gain[None]
            return c

        lax.fori_loop(0, frames // FB, fill, 0)

        def step(i, c):
            t = i * STEP
            acc = tapb[0, :, lanes][None] * spad[pl.ds(t, STEP)]
            for k in range(1, taps):
                acc = acc + tapb[k, :, lanes][None] * spad[pl.ds(t + k, STEP)]
            conv[pl.ds(t, STEP), :, lanes] = acc
            hidden[pl.ds(t, STEP), :, lanes] = (acc / (1.0 + jnp.exp(-acc))).astype(BF16)
            return c

        lax.fori_loop(0, frames // STEP, step, 0)
        return carry

    lax.fori_loop(0, chunks, convolve, 0)

    up2.wait_recv()
    down2.wait_recv()

    def column(d):
        return pl.ds(pl.multiple_of(peer_x[d] * width, LANES), width)

    pieces = [(dy_own, 0), (ring.at[0], shards - 1), (ring.at[1], 1), (ring.at[2], 2)]

    def hid_block(b, carry):
        acc = None
        for piece, d in pieces:
            rows = piece[pl.ds(b * (FB // 2), FB // 2)].reshape(FB * segs, width)
            term = lax.dot_general(
                rows, w_ref[:, column(d)], (((1,), (1,)), ((), ())), preferred_element_type=F32
            )
            acc = term if acc is None else acc + term
        hid[pl.ds(b * FB, FB)] = acc.reshape(FB, segs, width)
        return carry

    lax.fori_loop(0, frames // FB, hid_block, 0)

    sum_a[...] = jnp.zeros_like(sum_a)
    sum_b[...] = jnp.zeros_like(sum_b)

    def backward(lb, carry):
        lanes = pl.ds(pl.multiple_of(lb * LANES, LANES), LANES)
        gain = gain_ref[:, lanes].astype(F32)

        def fill(i, c):
            at = pl.ds(i * STEP, STEP)
            a = conv[at, :, lanes]
            s = 1.0 / (1.0 + jnp.exp(-a))
            gpad[pl.ds(i * STEP + half, STEP)] = hid[at, :, lanes] * s * (1.0 + a * (1.0 - s))
            spad[pl.ds(i * STEP + half, STEP)] = normed[at, :, lanes] * gain[None]
            return c

        lax.fori_loop(0, frames // STEP, fill, 0)

        def transposed(i, gain_sum):
            t = i * STEP
            at = pl.ds(t, STEP)
            acc = tapb[0, :, lanes][None] * gpad[pl.ds(t + taps - 1, STEP)]
            for k in range(1, taps):
                acc = acc + tapb[k, :, lanes][None] * gpad[pl.ds(t + taps - 1 - k, STEP)]
            hid[at, :, lanes] = acc
            cross = acc * normed[at, :, lanes]
            sum_a[at] = sum_a[at] + acc * gain[None]
            sum_b[at] = sum_b[at] + cross * gain[None]
            return gain_sum + jnp.sum(cross, axis=0)

        gain_sum = lax.fori_loop(0, frames // STEP, transposed, jnp.zeros((segs, LANES), F32))
        ggrad_ref[:, lanes] = jnp.sum(gain_sum, axis=0, keepdims=True) * grad_scale
        kacc[...] = jnp.zeros_like(kacc)

        def tap_sums(i, c):
            t = i * STEP
            g = gpad[pl.ds(t + half, STEP)]
            for k in range(taps):
                kacc[k] = kacc[k] + jnp.sum(g * spad[pl.ds(t + k, STEP)], axis=0)
            return c

        lax.fori_loop(0, frames // STEP, tap_sums, 0)
        for k in range(taps):
            kgrad_ref[k : k + 1, lanes] = jnp.sum(kacc[k], axis=0, keepdims=True) * grad_scale
        return carry

    lax.fori_loop(0, chunks, backward, 0)

    def sum_rows(b, carry):
        at = pl.ds(pl.multiple_of(b * FB, FB), FB)
        first = jnp.sum(sum_a[at], axis=2, keepdims=True)
        second = jnp.sum(sum_b[at], axis=2, keepdims=True)
        mom[1, at] = to_row(first, second, segs)
        return carry

    lax.fori_loop(0, frames // FB, sum_rows, 0)
    copies = exchange(mom.at[1], sums, 1)
    sent(s0, dy_own, 3)
    for copy in copies:
        copy.wait()

    def finish(b, carry):
        at = pl.ds(pl.multiple_of(b * FB, FB), FB)
        row = mom[1, at]
        for d in range(1, shards):
            row = row + sums[d, at]
        row = row * (1.0 / (shards * width))
        plain = to_column(row, segs)
        cross = to_column(pltpu.roll(row, LANES // 2, 1), segs)
        scale = scale_c[at][:, :, 0:1]
        ng = hid[at] * gain_ref[...].astype(F32)[None]
        branch = scale * (ng - plain - normed[at] * cross)
        dy = dy_own[pl.ds(b * (FB // 2), FB // 2)].astype(F32).reshape(FB, segs, width)
        s0[pl.ds(b * (FB // 2), FB // 2)] = (dy + branch).astype(BF16).reshape(FB // 2, 2, segs, width)
        return carry

    lax.fori_loop(0, frames // FB, finish, 0)
    scatter(s0, r0, 5)

    hidden_rows = hidden[...].reshape(frames * segs, width)
    for piece, d in pieces:
        rows = piece[...].reshape(frames * segs, width)
        block = lax.dot_general(hidden_rows, rows, (((0,), (0,)), ((), ())), preferred_element_type=F32)
        wgrad_ref[:, column(d)] = (block * grad_scale).astype(BF16)

    sent(s1, x_own, 4)
    arrived(s0, r0, 5)
    permute(pick_t, r0, s1)
    scatter(s1, r1, 6)
    sent(langs_own, langs_all, 0)
    for copy in (up, down, up2, down2):
        copy.wait_send()
    sent(s0, r0, 5)
    arrived(s1, r1, 6)

    def join_frames(b, carry):
        rows = r1[pl.ds(b * (FB // 2), FB // 2)].astype(F32).reshape(FB, segs, width)
        feat_ref[:, pl.ds(pl.multiple_of(b * FB, FB), FB), :] = jnp.swapaxes(rows, 0, 1).astype(BF16)
        return carry

    lax.fori_loop(0, frames // FB, join_frames, 0)
    sent(s1, r1, 6)


def per_device(feats, cotan, lang, w_out, gain, kernel):
    segs, frames, width = feats.shape
    owners = lax.axis_size("expert")
    shards = lax.axis_size("fsdp")
    taps = kernel.shape[1]
    total = owners * segs
    grad_scale = float(segs * frames) ** (-0.5)
    group = LANES // segs
    lane_owner = jnp.arange(LANES, dtype=jnp.int32) // segs
    here = lane_owner == lax.axis_index("expert") % group
    lang_row = jnp.where(here, jnp.tile(lang, group), 0).astype(F32)[None, :]

    shape = jax.ShapeDtypeStruct
    blocks = (owners, frames // owners, segs, width)
    f32_rows = pltpu.VMEM((frames, segs, width), F32)
    columns = pltpu.VMEM((frames, segs, LANES), F32)
    padded = pltpu.VMEM((frames + 32, segs, LANES), F32)
    dma = pltpu.SemaphoreType.DMA
    vmem = pl.BlockSpec(memory_space=pltpu.VMEM)
    feat_grad, w_grad, gain_grad, tap_grad = pl.pallas_call(
        functools.partial(module_kernel, owners, shards, grad_scale),
        out_shape=(
            shape((segs, frames, width), BF16),
            shape(w_out.shape[1:], BF16),
            shape((1, width), F32),
            shape((taps, width), F32),
        ),
        in_specs=[vmem] * 6,
        out_specs=(vmem,) * 4,
        scratch_shapes=[
            pltpu.VMEM((2, owners, 1, LANES), F32),
            *[pltpu.VMEM(blocks, BF16)] * 6,
            pltpu.VMEM((shards - 1,) + blocks, BF16),
            pltpu.VMEM((total, total), BF16),
            pltpu.VMEM((total, total), BF16),
            f32_rows,
            f32_rows,
            pltpu.VMEM((frames, segs, width), BF16),
            f32_rows,
            padded,
            padded,
            pltpu.VMEM((taps, segs, width), F32),
            pltpu.VMEM((taps, segs, LANES), F32),
            columns,
            columns,
            columns,
            pltpu.VMEM((2, frames, LANES), F32),
            pltpu.VMEM((shards, frames, LANES), F32),
            pltpu.VMEM((shards, frames, LANES), F32),
            dma((7,)),
            dma((7,)),
            dma((4,)),
            dma((4,)),
            dma((2, shards)),
            dma((2, shards)),
        ],
        compiler_params=pltpu.CompilerParams(
            collective_id=0, has_side_effects=True, vmem_limit_bytes=67043328
        ),
        name="module_backward",
    )(lang_row, feats, cotan, w_out[0], gain, kernel[0])
    return feat_grad, w_grad[None], gain_grad, tap_grad[None]


def solution(mesh):
    in_specs = (
        P("expert", None, "fsdp"),
        P("expert", None, "fsdp"),
        P("expert"),
        P("expert", "fsdp", None),
        P("expert", "fsdp"),
        P("expert", None, "fsdp"),
    )
    out_specs = (
        P("expert", None, "fsdp"),
        P("expert", "fsdp", None),
        P("expert", "fsdp"),
        P("expert", None, "fsdp"),
    )
    return jax.shard_map(
        per_device, mesh=mesh, in_specs=in_specs, out_specs=out_specs, check_vma=False
    )
```

time: 780 us -> 298 us (0.38); the launches traced: 768 us -> 297 us
  waiting for transfers between devices: 308 us -> 0 us
  Pallas kernels: 0 us -> 289 us
  local copies, waits for them, and re-layouts: 154 us -> 6.64 us
  other arithmetic: 137 us -> 0.52 us
  matrix products: 81.6 us -> 0 us
  starting transfers between devices: 44.5 us -> 0 us
  blocking collectives: 27.1 us -> 0 us
  between operations: 14.8 us -> 0.66 us
    all_to_all x4 -> x0, waiting for transfers between devices: 308 us -> none  [the longest x1 116 us: per_device(): lax.all_to_all(send_dy, 'expert', split_axis=0, concat_axis=0, tiled=True)]
    pallas_call x0 -> x1, Pallas kernels: none -> 289 us  [per_device(): pl.pallas_call(functools.partial(module_kernel, owners, shards, grad_scal...]
    unnamed x56 -> x8, local copies, waits for them, and re-layouts: 150 us -> 5.91 us
    reduce_sum x6 -> x0, other arithmetic: 87 us -> none  [the longest x1 53.3 us: back_split(): gain_grad = jnp.sum(scaled_grad * normed, axis=(0, 1))]
    dot_general x8 -> x0, matrix products: 81.6 us -> none  [the longest x1 27.7 us: per_device(): hid_sum = jnp.dot(shard_part, w_rows.T, preferred_element_type=jnp.float32)]
    all_to_all x4 -> x0, starting transfers between devices: 44.2 us -> none  [the longest x1 14.1 us: per_device(): lax.all_to_all(back_slots.reshape(owners, capacity, -1), 'expert', split_...]
    reshape x3 -> x0, other arithmetic: 27.3 us -> none  [the longest x1 9.11 us: per_device(): back_slots.reshape(owners, capacity, -1)]
    psum x3 -> x0, blocking collectives: 27.1 us -> none  [the longest x1 12.4 us: back_split(): lax.psum((jnp.sum(norm_grad, axis=-1), jnp.sum(norm_grad * normed, axis=-...]
  transfers between devices with their start and end apart: 5 -> 0, of which waited for: 3 -> 0; matrix products, arithmetic and copies ran while one was open for 27% -> 0% of each run, Pallas kernels for 0% -> 0%
where the time goes in v2:
time: 298 us; the launch traced here: 297 us
  Pallas kernels  289 us (97%)
  local copies, waits for them, and re-layouts  6.64 us (2%)
    pallas_call x1, Pallas kernels, per_device(): pl.pallas_call(functools.partial(module_kernel, owners, shards, grad_scal...  289 us

profile of v2, /device:TPU:1, one launch (start us, length us, event | category | flops | bytes accessed | tf_op | source)
XLA Modules:
  0.0 297.1 jit_solution(6023762086683874234)
XLA Ops:
  0.6 0.7 tile.4
  1.3 0.1 tile.10
  1.4 0.5 fusion.lang_ref
  1.9 289.3 %module_backward.1 = (bf16[16,128,384]{2,1,0:T(8,128)(2,1)}, bf16[384,1536]{1,0:T(8,128)(2,1)}, f32[1,384]{1,0:T(1,128)}, f32[31,384]{1,0:T(8,128)}) custom-call(f32[1,128]{1,0:T(1,128)} %fusion.lang_ref, bf16[16,128,384]{2,1,0:T(8,128)(2,1)} %x_ref.1, bf16[16,128,384]{2,1,0:T(8,128)(2,1)} %dy_ref.1, bf16[384,1536]{1,0:T(8,128)(2,1)} %bitcast.5, ...), custom_call_target="tpu_custom_call" | custom-call | tf_op jit(solution)/shard_map/module_backward/pallas_call | solution.py:403
  291.2 1.5 copy.10
  292.7 0.0 copy-start
  292.7 2.9 copy.14
  295.5 0.0 copy-done
  295.5 0.0 copy-start.1
  295.5 1.0 copy.15
  296.5 0.0 copy-done.1
  296.5 0.6 copy.16
Async XLA Ops:
  292.7 2.9 copy-start
  295.5 1.0 copy-start.1

commit v3 on v2

v3 whole, which is shorter than its diff:
```python
import functools

import jax
import jax.numpy as jnp
from jax import lax
from jax.experimental import pallas as pl
from jax.experimental.pallas import tpu as pltpu
from jax.sharding import PartitionSpec as P

MESH = pl.DeviceIdType.MESH
F32 = jnp.float32
BF16 = jnp.bfloat16
LANES = 128
STEP = 16
FB = 16


def diagonal(segs):
    lane = lax.broadcasted_iota(jnp.int32, (1, segs, LANES), 2)
    seg = lax.broadcasted_iota(jnp.int32, (1, segs, LANES), 1)
    return lane == seg, lane == seg + segs


def to_row(first, second, segs):
    low, high = diagonal(segs)
    spread = jnp.where(low, first, 0.0) + jnp.where(high, second, 0.0)
    return jnp.sum(spread, axis=1)


def to_column(row, segs):
    low, _ = diagonal(segs)
    return jnp.sum(jnp.where(low, row[:, None, :], 0.0), axis=2, keepdims=True)


def mean_and_scale(rows, width, segs):
    n = len(rows)
    squares = [pltpu.roll(r, LANES - segs, 1) for r in rows]
    mean = sum(rows) * (1.0 / n)
    spread = sum((r - mean) * (r - mean) for r in rows)
    var = (sum(squares) + width * spread) * (1.0 / (n * width))
    return mean, lax.rsqrt(var + 1e-05)


def module_kernel(
    owners, shards, grad_scale,
    lang_ref, x_ref, dy_ref, w_ref, gain_ref, taps_ref,
    feat_ref, wgrad_ref, ggrad_ref, kgrad_ref,
    langs, s0, s1, r0, r1, p_dy, p_x, own_dy, own_x, ring, back, pick, pick_t,
    normed, conv, hidden, hid, gpad, spad, tapb, kacc, gacc, sum_a, sum_b, scale_c, rows_a, rows_b, mom, parts,
    send, recv, ring_send, ring_recv, ex_send, ex_recv,
):
    all_segs, frames, width = x_ref.shape
    segs = own_x.shape[3]
    taps = taps_ref.shape[0]
    half = taps // 2
    total = owners * all_segs
    part = owners * segs
    chunks = width // LANES
    blocks = frames // FB
    me = lax.axis_index("expert")
    fs = lax.axis_index("fsdp")
    peer_x = [lax.rem(fs + d, shards) for d in range(shards)]

    barrier = pltpu.get_barrier_semaphore()

    def greet(d, carry):
        pl.semaphore_signal(
            barrier, inc=1, device_id={"expert": lax.rem(me + d, owners)}, device_id_type=MESH
        )
        return carry

    lax.fori_loop(1, owners, greet, 0)
    for d in range(1, shards):
        pl.semaphore_signal(barrier, inc=1, device_id={"fsdp": peer_x[d]}, device_id_type=MESH)

    def split_frames(src, dst):
        def block(b, carry):
            rows = src[:, pl.ds(pl.multiple_of(b * FB, FB), FB), :].astype(F32)
            moved = jnp.swapaxes(rows, 0, 1).astype(BF16)
            dst[pl.ds(b * (FB // 2), FB // 2)] = moved.reshape(FB // 2, 2, all_segs, width)
            return carry

        lax.fori_loop(0, blocks, block, 0)

    def scatter(src, dst, i):
        def one(p):
            pltpu.make_async_remote_copy(
                src_ref=src.at[p], dst_ref=dst.at[me], send_sem=send.at[i], recv_sem=recv.at[i],
                device_id={"expert": p}, device_id_type=MESH,
            ).start()

        def both(d, carry):
            one(lax.rem(me + d, owners))
            one(lax.rem(me + owners - d, owners))
            return carry

        lax.fori_loop(1, owners // 2, both, 0)
        one(lax.rem(me + owners // 2, owners))
        pltpu.make_async_copy(src.at[me], dst.at[me], recv.at[i]).start()

    def arrived(src, dst, i):
        pltpu.make_async_copy(src, dst, recv.at[i]).wait()

    def sent(src, dst, i):
        most = pl.ds(0, owners - 1)
        pltpu.make_async_remote_copy(
            src_ref=src.at[most], dst_ref=dst.at[most], send_sem=send.at[i], recv_sem=recv.at[i],
            device_id={"expert": lax.rem(me + 1, owners)}, device_id_type=MESH,
        ).wait_send()

    split_frames(dy_ref, s0)
    langs_own = langs.at[0]
    langs_all = langs.at[1]

    def spread_langs(d, carry):
        langs_own[d] = lang_ref[...]
        return carry

    lax.fori_loop(0, owners, spread_langs, 0)
    pl.semaphore_wait(barrier, owners - 1 + shards - 1)
    scatter(langs_own, langs_all, 0)
    scatter(s0, r0, 1)
    split_frames(x_ref, s1)
    scatter(s1, r1, 2)

    for k in range(taps):
        tapb[k] = jnp.broadcast_to(taps_ref[k : k + 1, :].astype(F32), (segs, width))
    for pad in (gpad, spad):
        pad[:half] = jnp.zeros((half, segs, LANES), F32)
        pad[half + frames :] = jnp.zeros((pad.shape[0] - half - frames, segs, LANES), F32)
    kacc[...] = jnp.zeros_like(kacc)
    gacc[...] = jnp.zeros_like(gacc)

    arrived(langs_own, langs_all, 0)
    owner_of = lax.broadcasted_iota(jnp.int32, (owners, LANES), 0).astype(F32)
    before = lax.broadcasted_iota(jnp.int32, (LANES, LANES), 0) < lax.broadcasted_iota(
        jnp.int32, (LANES, LANES), 1
    )
    before = jnp.where(before, 1.0, 0.0).astype(BF16)
    place = lax.broadcasted_iota(jnp.int32, (total, LANES), 0).astype(F32)
    base = jnp.zeros((owners, 1), F32)
    group = LANES // all_segs
    for q in range(total // LANES):
        row = jnp.sum(langs_all[q * group : (q + 1) * group], axis=0)
        match = jnp.where(owner_of == row, 1.0, 0.0)
        rank = jnp.dot(match.astype(BF16), before, preferred_element_type=F32) + base
        base = base + jnp.sum(match, axis=1, keepdims=True)
        spot = owner_of * segs + rank + jnp.where(rank >= segs, float(part - segs), 0.0)
        dest = jnp.sum(match * spot, axis=0, keepdims=True)
        pick[:, q * LANES : (q + 1) * LANES] = jnp.where(place == dest, 1.0, 0.0).astype(BF16)
    number = lax.broadcasted_iota(jnp.int32, (16, total), 1)
    which = lax.broadcasted_iota(jnp.int32, (16, total), 0)
    digits = jnp.where(which == 0, number // 32, number % 32).astype(F32).astype(BF16)
    found = lax.dot_general(digits, pick[...], (((1,), (1,)), ((), ())), preferred_element_type=F32)
    source = found[0:1] * 32.0 + found[1:2]
    for q in range(total // LANES):
        cols = slice(q * LANES, (q + 1) * LANES)
        pick_t[:, cols] = jnp.where(place == source[:, cols], 1.0, 0.0).astype(BF16)

    def permute_out(h, src, dst):
        rows = 256

        def block(b, carry):
            choice = pick[pl.ds(pl.multiple_of(h * part + b * rows, rows), rows), :]
            for j in range(2):
                flat = src[:, j].reshape(total, width)
                moved = jnp.dot(choice, flat, preferred_element_type=F32).astype(BF16)
                dst[pl.ds(b * (rows // segs), rows // segs), j] = moved.reshape(rows // segs, segs, width)
            return carry

        lax.fori_loop(0, part // rows, block, 0)

    def permute_home(dst):
        rows = 256

        def block(b, carry):
            at = pl.ds(pl.multiple_of(b * rows, rows), rows)
            for j in range(2):
                moved = None
                for h in range(2):
                    flat = back[h, :, j].reshape(part, width)
                    term = jnp.dot(pick_t[at, h * part : (h + 1) * part], flat, preferred_element_type=F32)
                    moved = term if moved is None else moved + term
                moved = moved.astype(BF16).reshape(rows // all_segs, all_segs, width)
                dst[pl.ds(b * (rows // all_segs), rows // all_segs), j] = moved
            return carry

        lax.fori_loop(0, total // rows, block, 0)

    arrived(s0, r0, 1)
    permute_out(0, r0, p_dy.at[0])
    scatter(p_dy.at[0], own_dy.at[0], 3)
    permute_out(1, r0, p_dy.at[1])
    arrived(s1, r1, 2)
    permute_out(0, r1, p_x.at[0])
    scatter(p_x.at[0], own_x.at[0], 4)
    scatter(p_dy.at[1], own_dy.at[1], 5)
    permute_out(1, r1, p_x.at[1])
    scatter(p_x.at[1], own_x.at[1], 6)

    def ring_copy(h, src, dst, i, d):
        return pltpu.make_async_remote_copy(
            src_ref=src, dst_ref=dst, send_sem=ring_send.at[h, i], recv_sem=ring_recv.at[h, i],
            device_id={"fsdp": peer_x[d]}, device_id_type=MESH,
        )

    middle = owners // 2

    def ring_copies(h):
        one = ring.at[h, 0]
        two = ring.at[h, 1]
        far = ring.at[h, 2]
        low = pl.ds(0, middle)
        high = pl.ds(middle, middle)
        return [
            ring_copy(h, own_dy.at[h], one, 0, 1),
            ring_copy(h, own_dy.at[h], two, 1, shards - 1),
            ring_copy(h, one.at[low], far.at[low], 2, 1),
            ring_copy(h, two.at[high], far.at[high], 3, shards - 1),
        ]

    rings = [ring_copies(0), ring_copies(1)]

    def start_ring(h):
        arrived(p_dy.at[h], own_dy.at[h], 3 + 2 * h)
        rings[h][0].start()
        rings[h][1].start()

    def exchange(i):
        copies = [
            pltpu.make_async_remote_copy(
                src_ref=mom.at[i], dst_ref=parts.at[i, d], send_sem=ex_send.at[i, d],
                recv_sem=ex_recv.at[i, d], device_id={"fsdp": peer_x[d]}, device_id_type=MESH,
            )
            for d in range(1, shards)
        ]
        for copy in copies:
            copy.start()
        return copies

    def gathered(i):
        return [mom[i]] + [parts[i, d] for d in range(1, shards)]

    def pack():
        packed = rows_a[0]
        for b in range(1, blocks):
            packed = packed + pltpu.roll(rows_a[b], 2 * segs * b, 1)
        return packed

    def unpack(packed, dst):
        dst[0] = packed
        for b in range(1, blocks):
            dst[b] = pltpu.roll(packed, LANES - 2 * segs * b, 1)

    def column(d):
        return pl.ds(pl.multiple_of(peer_x[d] * width, LANES), width)

    def pieces(h):
        return [
            (own_dy.at[h], 0), (ring.at[h, 0], shards - 1), (ring.at[h, 1], 1), (ring.at[h, 2], 2)
        ]

    def stage(h, between):
        dy = own_dy.at[h]
        x_own = own_x.at[h]
        arrived(p_x.at[h], x_own, 4 + 2 * h)

        def moments(b, carry):
            x = x_own[pl.ds(b * (FB // 2), FB // 2)].astype(F32).reshape(FB, segs, width)
            mean = jnp.sum(x, axis=2, keepdims=True) * (1.0 / width)
            centre = x - mean
            square = jnp.sum(centre * centre, axis=2, keepdims=True)
            rows_a[b] = to_row(mean, square, segs)
            return carry

        lax.fori_loop(0, blocks, moments, 0)
        mom[2 * h] = pack()
        copies = exchange(2 * h)
        up, down, up2, down2 = rings[h]
        up.wait_recv()
        down.wait_recv()
        up2.start()
        down2.start()
        for copy in copies:
            copy.wait()
        mean_row, scale_row = mean_and_scale(gathered(2 * h), width, segs)
        unpack(mean_row, rows_a)
        unpack(scale_row, rows_b)

        def normalize(b, carry):
            at = pl.ds(b * FB, FB)
            mean = to_column(rows_a[b], segs)
            scale = to_column(rows_b[b], segs)
            x = x_own[pl.ds(b * (FB // 2), FB // 2)].astype(F32).reshape(FB, segs, width)
            normed[at] = (x - mean) * scale
            scale_c[at] = jnp.broadcast_to(scale, (FB, segs, LANES))
            return carry

        lax.fori_loop(0, blocks, normalize, 0)

        def convolve(lb, carry):
            lanes = pl.ds(pl.multiple_of(lb * LANES, LANES), LANES)
            gain = gain_ref[:, lanes].astype(F32)

            def fill(i, c):
                at = pl.ds(i * FB, FB)
                spad[pl.ds(i * FB + half, FB)] = normed[at, :, lanes] * gain[None]
                return c

            lax.fori_loop(0, blocks, fill, 0)

            def step(i, c):
                t = i * STEP
                acc = tapb[0, :, lanes][None] * spad[pl.ds(t, STEP)]
                for k in range(1, taps):
                    acc = acc + tapb[k, :, lanes][None] * spad[pl.ds(t + k, STEP)]
                conv[pl.ds(t, STEP), :, lanes] = acc
                hidden[h, pl.ds(t, STEP), :, lanes] = (acc / (1.0 + jnp.exp(-acc))).astype(BF16)
                return c

            lax.fori_loop(0, frames // STEP, step, 0)
            return carry

        lax.fori_loop(0, chunks, convolve, 0)
        up2.wait_recv()
        down2.wait_recv()

        def hid_block(b, carry):
            acc = None
            for piece, d in pieces(h):
                rows = piece[pl.ds(b * FB, FB)].reshape(2 * FB * segs, width)
                term = lax.dot_general(
                    rows, w_ref[:, column(d)], (((1,), (1,)), ((), ())), preferred_element_type=F32
                )
                acc = term if acc is None else acc + term
            hid[pl.ds(b * 2 * FB, 2 * FB)] = acc.reshape(2 * FB, segs, width)
            return carry

        lax.fori_loop(0, blocks // 2, hid_block, 0)
        sum_a[...] = jnp.zeros_like(sum_a)
        sum_b[...] = jnp.zeros_like(sum_b)

        def backward(lb, carry):
            lanes = pl.ds(pl.multiple_of(lb * LANES, LANES), LANES)
            gain = gain_ref[:, lanes].astype(F32)

            def fill(i, c):
                at = pl.ds(i * STEP, STEP)
                a = conv[at, :, lanes]
                s = 1.0 / (1.0 + jnp.exp(-a))
                gpad[pl.ds(i * STEP + half, STEP)] = hid[at, :, lanes] * s * (1.0 + a * (1.0 - s))
                spad[pl.ds(i * STEP + half, STEP)] = normed[at, :, lanes] * gain[None]
                return c

            lax.fori_loop(0, frames // STEP, fill, 0)

            def transposed(i, gain_sum):
                t = i * STEP
                at = pl.ds(t, STEP)
                acc = tapb[0, :, lanes][None] * gpad[pl.ds(t + taps - 1, STEP)]
                for k in range(1, taps):
                    acc = acc + tapb[k, :, lanes][None] * gpad[pl.ds(t + taps - 1 - k, STEP)]
                hid[at, :, lanes] = acc
                cross = acc * normed[at, :, lanes]
                sum_a[at] = sum_a[at] + acc * gain[None]
                sum_b[at] = sum_b[at] + cross * gain[None]
                return gain_sum + jnp.sum(cross, axis=0)

            zero = jnp.zeros((segs, LANES), F32)
            gacc[:, lanes] = gacc[:, lanes] + lax.fori_loop(0, frames // STEP, transposed, zero)

            def tap_sums(i, c):
                t = i * STEP
                g = gpad[pl.ds(t + half, STEP)]
                for k in range(taps):
                    kacc[k, :, lanes] = kacc[k, :, lanes] + jnp.sum(g * spad[pl.ds(t + k, STEP)], axis=0)
                return c

            lax.fori_loop(0, frames // STEP, tap_sums, 0)
            return carry

        lax.fori_loop(0, chunks - 1, backward, 0)
        between()
        lax.fori_loop(chunks - 1, chunks, backward, 0)

        def sum_rows(b, carry):
            at = pl.ds(b * FB, FB)
            first = jnp.sum(sum_a[at], axis=2, keepdims=True)
            second = jnp.sum(sum_b[at], axis=2, keepdims=True)
            rows_a[b] = to_row(first, second, segs)
            return carry

        lax.fori_loop(0, blocks, sum_rows, 0)
        mom[2 * h + 1] = pack()
        copies = exchange(2 * h + 1)
        sent(p_dy.at[h], dy, 3 + 2 * h)
        for copy in copies:
            copy.wait()
        row = sum(gathered(2 * h + 1)) * (1.0 / (shards * width))
        unpack(row, rows_a)
        unpack(pltpu.roll(row, LANES - segs, 1), rows_b)

        def finish(b, carry):
            at = pl.ds(b * FB, FB)
            plain = to_column(rows_a[b], segs)
            cross = to_column(rows_b[b], segs)
            scale = scale_c[at][:, :, 0:1]
            ng = hid[at] * gain_ref[...].astype(F32)[None]
            branch = scale * (ng - plain - normed[at] * cross)
            grads = dy[pl.ds(b * (FB // 2), FB // 2)].astype(F32).reshape(FB, segs, width)
            p_dy[h, pl.ds(b * (FB // 2), FB // 2)] = (
                (grads + branch).astype(BF16).reshape(FB // 2, 2, segs, width)
            )
            return carry

        lax.fori_loop(0, blocks, finish, 0)
        scatter(p_dy.at[h], back.at[h], 7 + h)

    start_ring(0)
    stage(0, lambda: start_ring(1))
    stage(1, lambda: None)

    for k in range(taps):
        kgrad_ref[k] = jnp.sum(kacc[k], axis=0, keepdims=True) * grad_scale
    ggrad_ref[...] = jnp.sum(gacc[...], axis=0, keepdims=True) * grad_scale
    rows_of = frames * segs
    for j in range(shards):
        block = None
        for h in range(2):
            piece, d = pieces(h)[j]
            term = lax.dot_general(
                hidden[h].reshape(rows_of, width), piece[...].reshape(rows_of, width),
                (((0,), (0,)), ((), ())), preferred_element_type=F32,
            )
            block = term if block is None else block + term
        wgrad_ref[:, column(d)] = (block * grad_scale).astype(BF16)

    sent(s0, r0, 1)
    arrived(p_dy.at[0], back.at[0], 7)
    arrived(p_dy.at[1], back.at[1], 8)
    permute_home(s0)
    scatter(s0, r0, 9)
    sent(langs_own, langs_all, 0)
    sent(s1, r1, 2)
    for h in range(2):
        sent(p_x.at[h], own_x.at[h], 4 + 2 * h)
        sent(p_dy.at[h], back.at[h], 7 + h)
        for copy in rings[h]:
            copy.wait_send()
    arrived(s0, r0, 9)

    def join_frames(b, carry):
        rows = r0[pl.ds(b * (FB // 2), FB // 2)].astype(F32).reshape(FB, all_segs, width)
        feat_ref[:, pl.ds(pl.multiple_of(b * FB, FB), FB), :] = jnp.swapaxes(rows, 0, 1).astype(BF16)
        return carry

    lax.fori_loop(0, blocks, join_frames, 0)
    sent(s0, r0, 9)


def per_device(feats, cotan, lang, w_out, gain, kernel):
    segs, frames, width = feats.shape
    owners = lax.axis_size("expert")
    shards = lax.axis_size("fsdp")
    taps = kernel.shape[1]
    total = owners * segs
    grad_scale = float(segs * frames) ** (-0.5)
    group = LANES // segs
    lane_owner = jnp.arange(LANES, dtype=jnp.int32) // segs
    here = lane_owner == lax.axis_index("expert") % group
    lang_row = jnp.where(here, jnp.tile(lang, group), 0).astype(F32)[None, :]

    shape = jax.ShapeDtypeStruct
    half = segs // 2
    whole = pltpu.VMEM((owners, frames // owners, segs, width), BF16)
    halves = (owners, frames // owners, half, width)
    f32_rows = pltpu.VMEM((frames, half, width), F32)
    columns = pltpu.VMEM((frames, half, LANES), F32)
    padded = pltpu.VMEM((frames + 32, half, LANES), F32)
    rows = pltpu.VMEM((frames // FB, FB, LANES), F32)
    dma = pltpu.SemaphoreType.DMA
    vmem = pl.BlockSpec(memory_space=pltpu.VMEM)
    feat_grad, w_grad, gain_grad, tap_grad = pl.pallas_call(
        functools.partial(module_kernel, owners, shards, grad_scale),
        out_shape=(
            shape((segs, frames, width), BF16),
            shape(w_out.shape[1:], BF16),
            shape((1, width), F32),
            shape((taps, 1, width), F32),
        ),
        in_specs=[vmem] * 6,
        out_specs=(vmem,) * 4,
        scratch_shapes=[
            pltpu.VMEM((2, owners, 1, LANES), F32),
            *[whole] * 4,
            *[pltpu.VMEM((2,) + halves, BF16)] * 4,
            pltpu.VMEM((2, shards - 1) + halves, BF16),
            pltpu.VMEM((2,) + halves, BF16),
            pltpu.VMEM((total, total), BF16),
            pltpu.VMEM((total, total), BF16),
            f32_rows,
            f32_rows,
            pltpu.VMEM((2, frames, half, width), BF16),
            f32_rows,
            padded,
            padded,
            pltpu.VMEM((taps, half, width), F32),
            pltpu.VMEM((taps, half, width), F32),
            pltpu.VMEM((half, width), F32),
            columns,
            columns,
            columns,
            rows,
            rows,
            pltpu.VMEM((4, FB, LANES), F32),
            pltpu.VMEM((4, shards, FB, LANES), F32),
            dma((10,)),
            dma((10,)),
            dma((2, 4)),
            dma((2, 4)),
            dma((4, shards)),
            dma((4, shards)),
        ],
        compiler_params=pltpu.CompilerParams(
            collective_id=0, has_side_effects=True, vmem_limit_bytes=67043328
        ),
        name="module_backward",
    )(lang_row, feats, cotan, w_out[0], gain, kernel[0])
    return feat_grad, w_grad[None], gain_grad, jnp.swapaxes(tap_grad, 0, 1)


def solution(mesh):
    in_specs = (
        P("expert", None, "fsdp"),
        P("expert", None, "fsdp"),
        P("expert"),
        P("expert", "fsdp", None),
        P("expert", "fsdp"),
        P("expert", None, "fsdp"),
    )
    out_specs = (
        P("expert", None, "fsdp"),
        P("expert", "fsdp", None),
        P("expert", "fsdp"),
        P("expert", None, "fsdp"),
    )
    return jax.shard_map(
        per_device, mesh=mesh, in_specs=in_specs, out_specs=out_specs, check_vma=False
    )
```

time: 298 us -> 260 us (0.87)
  Pallas kernels: 289 us -> 253 us
    pallas_call x1, Pallas kernels: 289 us -> 253 us  [per_device(): pl.pallas_call(functools.partial(module_kernel, owners, shards, grad_scal...]
where the time goes in v3:
time: 260 us
  Pallas kernels  253 us (97%)
  local copies, waits for them, and re-layouts  5.8 us (2%)
    pallas_call x1, Pallas kernels, per_device(): pl.pallas_call(functools.partial(module_kernel, owners, shards, grad_scal...  253 us

profile of v3, /device:TPU:1, one launch (start us, length us, event | category | flops | bytes accessed | tf_op | source)
XLA Modules:
  0.0 260.0 jit_solution(3529056272448045356)
XLA Ops:
  0.6 0.7 tile.4
  1.3 0.1 tile.10
  1.4 0.5 fusion.lang_ref
  1.9 253.0 %module_backward.1 = (bf16[16,128,384]{2,1,0:T(8,128)(2,1)}, bf16[384,1536]{1,0:T(8,128)(2,1)}, f32[1,384]{1,0:T(1,128)}, f32[31,1,384]{2,1,0:T(1,128)}) custom-call(f32[1,128]{1,0:T(1,128)} %fusion.lang_ref, bf16[16,128,384]{2,1,0:T(8,128)(2,1)} %x_ref.1, bf16[16,128,384]{2,1,0:T(8,128)(2,1)} %dy_ref.1, bf16[384,1536]{1,0:T(8,128)(2,1)} %bitcast.5, ...), custom_call_target="tpu_custom_call" | custom-call | tf_op jit(solution)/shard_map/module_backward/pallas_call | solution.py:483
  254.9 0.0 copy-start
  254.9 2.9 %copy.14 = bf16[16,128,384]{2,1,0:T(8,128)(2,1)} copy(bf16[16,128,384]{2,1,0:T(8,128)(2,1)} %get-tuple-element.16) | data formatting | bytes 3145728
  257.8 0.0 copy-done
  257.8 0.0 copy-start.2
  257.8 0.0 copy-start.1
  257.8 1.0 copy.15
  258.8 0.0 copy-done.2
  258.8 0.6 copy.16
  259.4 0.0 copy-done.1
  259.4 0.6 copy.17
Async XLA Ops:
  254.9 2.9 %copy-start = (bf16[384,1536]{1,0:T(8,128)(2,1)S(1)}, bf16[384,1536]{1,0:T(8,128)(2,1)}, u32[]{:S(2)}) copy-start(bf16[384,1536]{1,0:T(8,128)(2,1)} %get-tuple-element.9) | copy-start | bytes 3538948
  257.8 1.0 copy-start.2
  257.8 1.6 copy-start.1

commit v4 on v3

--- a/solution.py
+++ b/solution.py
@@ -44,10 +44,10 @@
 def module_kernel(
     owners, shards, grad_scale,
     lang_ref, x_ref, dy_ref, w_ref, gain_ref, taps_ref,
-    feat_ref, wgrad_ref, ggrad_ref, kgrad_ref,
-    langs, s0, s1, r0, r1, p_dy, p_x, own_dy, own_x, ring, back, pick, pick_t,
+    home_ref, wgrad_ref, ggrad_ref, kgrad_ref,
+    x_vmem, dy_vmem, w_vmem, langs, s0, s1, r0, r1, p_dy, p_x, own_dy, own_x, ring, ret, back, home, pick, pick_t,
     normed, conv, hidden, hid, gpad, spad, tapb, kacc, gacc, sum_a, sum_b, scale_c, rows_a, rows_b, mom, parts,
-    send, recv, ring_send, ring_recv, ex_send, ex_recv,
+    send, recv, ring_send, ring_recv, ex_send, ex_recv, load,
 ):
     all_segs, frames, width = x_ref.shape
     segs = own_x.shape[3]
@@ -69,6 +69,12 @@
         )
         return carry
 
+    loads = [
+        pltpu.make_async_copy(src, dst, load.at[i])
+        for i, (src, dst) in enumerate(((dy_ref, dy_vmem), (x_ref, x_vmem), (w_ref, w_vmem)))
+    ]
+    for copy in loads:
+        copy.start()
     lax.fori_loop(1, owners, greet, 0)
     for d in range(1, shards):
         pl.semaphore_signal(barrier, inc=1, device_id={"fsdp": peer_x[d]}, device_id_type=MESH)
@@ -108,19 +114,27 @@
             device_id={"expert": lax.rem(me + 1, owners)}, device_id_type=MESH,
         ).wait_send()
 
-    split_frames(dy_ref, s0)
+    lane = lax.broadcasted_iota(jnp.int32, (1, LANES), 1)
+    first_lane = lax.rem(me, LANES // all_segs) * all_segs
+    lang_row = jnp.zeros((1, LANES), jnp.int32)
+    for i in range(all_segs):
+        lang_row = jnp.where(lane == first_lane + i, lang_ref[i], lang_row)
+    lang_row = lang_row.astype(F32)
+    loads[0].wait()
+    split_frames(dy_vmem, s0)
     langs_own = langs.at[0]
     langs_all = langs.at[1]
 
     def spread_langs(d, carry):
-        langs_own[d] = lang_ref[...]
+        langs_own[d] = lang_row
         return carry
 
     lax.fori_loop(0, owners, spread_langs, 0)
     pl.semaphore_wait(barrier, owners - 1 + shards - 1)
     scatter(langs_own, langs_all, 0)
     scatter(s0, r0, 1)
-    split_frames(x_ref, s1)
+    loads[1].wait()
+    split_frames(x_vmem, s1)
     scatter(s1, r1, 2)
 
     for k in range(taps):
@@ -170,19 +184,18 @@
 
         lax.fori_loop(0, part // rows, block, 0)
 
-    def permute_home(dst):
+    def permute_home(j, dst):
         rows = 256
 
         def block(b, carry):
             at = pl.ds(pl.multiple_of(b * rows, rows), rows)
-            for j in range(2):
-                moved = None
-                for h in range(2):
-                    flat = back[h, :, j].reshape(part, width)
-                    term = jnp.dot(pick_t[at, h * part : (h + 1) * part], flat, preferred_element_type=F32)
-                    moved = term if moved is None else moved + term
-                moved = moved.astype(BF16).reshape(rows // all_segs, all_segs, width)
-                dst[pl.ds(b * (rows // all_segs), rows // all_segs), j] = moved
+            moved = None
+            for h in range(2):
+                flat = back[h, j].reshape(part, width)
+                term = jnp.dot(pick_t[at, h * part : (h + 1) * part], flat, preferred_element_type=F32)
+                moved = term if moved is None else moved + term
+            moved = moved.astype(BF16).reshape(rows // all_segs, all_segs, width)
+            dst[pl.ds(b * (rows // all_segs), rows // all_segs)] = moved
             return carry
 
         lax.fori_loop(0, total // rows, block, 0)
@@ -207,16 +220,19 @@
     middle = owners // 2
 
     def ring_copies(h):
+        own = own_dy.at[h]
         one = ring.at[h, 0]
         two = ring.at[h, 1]
         far = ring.at[h, 2]
         low = pl.ds(0, middle)
         high = pl.ds(middle, middle)
         return [
-            ring_copy(h, own_dy.at[h], one, 0, 1),
-            ring_copy(h, own_dy.at[h], two, 1, shards - 1),
-            ring_copy(h, one.at[low], far.at[low], 2, 1),
-            ring_copy(h, two.at[high], far.at[high], 3, shards - 1),
+            ring_copy(h, own.at[low], one.at[low], 0, 1),
+            ring_copy(h, own.at[high], two.at[high], 1, shards - 1),
+            ring_copy(h, own.at[high], one.at[high], 2, 1),
+            ring_copy(h, own.at[low], two.at[low], 3, shards - 1),
+            ring_copy(h, one.at[low], far.at[low], 4, 1),
+            ring_copy(h, two.at[high], far.at[high], 5, shards - 1),
         ]
 
     rings = [ring_copies(0), ring_copies(1)]
@@ -225,6 +241,10 @@
         arrived(p_dy.at[h], own_dy.at[h], 3 + 2 * h)
         rings[h][0].start()
         rings[h][1].start()
+
+    def go_on_ring(h):
+        rings[h][2].start()
+        rings[h][3].start()
 
     def exchange(i):
         copies = [
@@ -260,7 +280,7 @@
             (own_dy.at[h], 0), (ring.at[h, 0], shards - 1), (ring.at[h, 1], 1), (ring.at[h, 2], 2)
         ]
 
-    def stage(h, between):
+    def stage(h, between, after):
         dy = own_dy.at[h]
         x_own = own_x.at[h]
         arrived(p_x.at[h], x_own, 4 + 2 * h)
@@ -276,11 +296,31 @@
         lax.fori_loop(0, blocks, moments, 0)
         mom[2 * h] = pack()
         copies = exchange(2 * h)
-        up, down, up2, down2 = rings[h]
-        up.wait_recv()
-        down.wait_recv()
-        up2.start()
-        down2.start()
+        for copy in rings[h][:4]:
+            copy.wait_recv()
+        rings[h][4].start()
+        rings[h][5].start()
+
+        def hid_rows(b, chosen):
+            acc = None
+            for piece, d in chosen:
+                rows = piece[pl.ds(b * FB, FB)].reshape(2 * FB * segs, width)
+                term = lax.dot_general(
+                    rows, w_vmem[:, column(d)], (((1,), (1,)), ((), ())), preferred_element_type=F32
+                )
+                acc = term if acc is None else acc + term
+            return acc.reshape(2 * FB, segs, width)
+
+        def hid_near(b, carry):
+            hid[pl.ds(b * 2 * FB, 2 * FB)] = hid_rows(b, pieces(h)[:3])
+            return carry
+
+        def hid_far(b, carry):
+            at = pl.ds(b * 2 * FB, 2 * FB)
+            hid[at] = hid[at] + hid_rows(b, pieces(h)[3:])
+            return carry
+
+        lax.fori_loop(0, blocks // 2, hid_near, 0)
         for copy in copies:
             copy.wait()
         mean_row, scale_row = mean_and_scale(gathered(2 * h), width, segs)
@@ -322,21 +362,10 @@
             return carry
 
         lax.fori_loop(0, chunks, convolve, 0)
-        up2.wait_recv()
-        down2.wait_recv()
-
-        def hid_block(b, carry):
-            acc = None
-            for piece, d in pieces(h):
-                rows = piece[pl.ds(b * FB, FB)].reshape(2 * FB * segs, width)
-                term = lax.dot_general(
-                    rows, w_ref[:, column(d)], (((1,), (1,)), ((), ())), preferred_element_type=F32
-                )
-                acc = term if acc is None else acc + term
-            hid[pl.ds(b * 2 * FB, 2 * FB)] = acc.reshape(2 * FB, segs, width)
-            return carry
-
-        lax.fori_loop(0, blocks // 2, hid_block, 0)
+        rings[h][4].wait_recv()
+        rings[h][5].wait_recv()
+        lax.fori_loop(0, blocks // 2, hid_far, 0)
+        between()
         sum_a[...] = jnp.zeros_like(sum_a)
         sum_b[...] = jnp.zeros_like(sum_b)
 
@@ -379,9 +408,7 @@
             lax.fori_loop(0, frames // STEP, tap_sums, 0)
             return carry
 
-        lax.fori_loop(0, chunks - 1, backward, 0)
-        between()
-        lax.fori_loop(chunks - 1, chunks, backward, 0)
+        lax.fori_loop(0, chunks, backward, 0)
 
         def sum_rows(b, carry):
             at = pl.ds(b * FB, FB)
@@ -393,7 +420,17 @@
         lax.fori_loop(0, blocks, sum_rows, 0)
         mom[2 * h + 1] = pack()
         copies = exchange(2 * h + 1)
-        sent(p_dy.at[h], dy, 3 + 2 * h)
+        after()
+
+        def prepare(b, carry):
+            at = pl.ds(b * FB, FB)
+            scale = scale_c[at][:, :, 0:1]
+            grads = dy[pl.ds(b * (FB // 2), FB // 2)].astype(F32).reshape(FB, segs, width)
+            hid[at] = grads + scale * (hid[at] * gain_ref[...].astype(F32)[None])
+            normed[at] = scale * normed[at]
+            return carry
+
+        lax.fori_loop(0, blocks, prepare, 0)
         for copy in copies:
             copy.wait()
         row = sum(gathered(2 * h + 1)) * (1.0 / (shards * width))
@@ -405,57 +442,73 @@
             plain = to_column(rows_a[b], segs)
             cross = to_column(rows_b[b], segs)
             scale = scale_c[at][:, :, 0:1]
-            ng = hid[at] * gain_ref[...].astype(F32)[None]
-            branch = scale * (ng - plain - normed[at] * cross)
-            grads = dy[pl.ds(b * (FB // 2), FB // 2)].astype(F32).reshape(FB, segs, width)
-            p_dy[h, pl.ds(b * (FB // 2), FB // 2)] = (
-                (grads + branch).astype(BF16).reshape(FB // 2, 2, segs, width)
-            )
+            out = (hid[at] - scale * plain - normed[at] * cross).astype(BF16)
+            out = out.reshape(FB // 2, 2, segs, width)
+            for j in range(2):
+                ret[h, j, pl.ds(b * (FB // 2), FB // 2)] = out[:, j]
             return carry
 
         lax.fori_loop(0, blocks, finish, 0)
-        scatter(p_dy.at[h], back.at[h], 7 + h)
-
+        for j in range(2):
+            scatter(ret.at[h, j], back.at[h, j], 7 + 2 * h + j)
+
+    loads[2].wait()
     start_ring(0)
-    stage(0, lambda: start_ring(1))
-    stage(1, lambda: None)
-
-    for k in range(taps):
-        kgrad_ref[k] = jnp.sum(kacc[k], axis=0, keepdims=True) * grad_scale
-    ggrad_ref[...] = jnp.sum(gacc[...], axis=0, keepdims=True) * grad_scale
-    rows_of = frames * segs
-    for j in range(shards):
-        block = None
+    go_on_ring(0)
+    stage(0, lambda: start_ring(1), lambda: go_on_ring(1))
+    stage(1, lambda: None, lambda: None)
+
+    def weights():
+        for k in range(taps):
+            kgrad_ref[k] = jnp.sum(kacc[k], axis=0, keepdims=True)
+        ggrad_ref[...] = jnp.sum(gacc[...], axis=0, keepdims=True)
+        rows_of = frames * segs
+        for j in range(shards):
+            block = None
+            for h in range(2):
+                piece, d = pieces(h)[j]
+                term = lax.dot_general(
+                    hidden[h].reshape(rows_of, width), piece[...].reshape(rows_of, width),
+                    (((0,), (0,)), ((), ())), preferred_element_type=F32,
+                )
+                block = term if block is None else block + term
+            wgrad_ref[:, column(d)] = (block * grad_scale).astype(BF16)
+
+    weights()
+    sent(s0, r0, 1)
+    for j in range(2):
         for h in range(2):
-            piece, d = pieces(h)[j]
-            term = lax.dot_general(
-                hidden[h].reshape(rows_of, width), piece[...].reshape(rows_of, width),
-                (((0,), (0,)), ((), ())), preferred_element_type=F32,
-            )
-            block = term if block is None else block + term
-        wgrad_ref[:, column(d)] = (block * grad_scale).astype(BF16)
-
-    sent(s0, r0, 1)
-    arrived(p_dy.at[0], back.at[0], 7)
-    arrived(p_dy.at[1], back.at[1], 8)
-    permute_home(s0)
-    scatter(s0, r0, 9)
+            arrived(ret.at[h, j], back.at[h, j], 7 + 2 * h + j)
+        permute_home(j, home.at[j])
+        scatter(home.at[j], home_ref.at[j], 11 + j)
     sent(langs_own, langs_all, 0)
     sent(s1, r1, 2)
     for h in range(2):
+        sent(p_dy.at[h], own_dy.at[h], 3 + 2 * h)
         sent(p_x.at[h], own_x.at[h], 4 + 2 * h)
-        sent(p_dy.at[h], back.at[h], 7 + h)
+        for j in range(2):
+            sent(ret.at[h, j], back.at[h, j], 7 + 2 * h + j)
         for copy in rings[h]:
             copy.wait_send()
-    arrived(s0, r0, 9)
+    for j in range(2):
+        arrived(home.at[j], home_ref.at[j], 11 + j)
+        sent(home.at[j], home_ref.at[j], 11 + j)
+
+
+def deliver_kernel(grad_scale, home_ref, w_ref, g_ref, k_ref, feat_ref, wgrad_ref, ggrad_ref, kgrad_ref):
+    segs, frames, width = feat_ref.shape
 
     def join_frames(b, carry):
-        rows = r0[pl.ds(b * (FB // 2), FB // 2)].astype(F32).reshape(FB, all_segs, width)
+        at = pl.ds(b * (FB // 2), FB // 2)
+        rows = jnp.stack([home_ref[0, at].astype(F32), home_ref[1, at].astype(F32)], axis=1)
+        rows = rows.reshape(FB, segs, width)
         feat_ref[:, pl.ds(pl.multiple_of(b * FB, FB), FB), :] = jnp.swapaxes(rows, 0, 1).astype(BF16)
         return carry
 
-    lax.fori_loop(0, blocks, join_frames, 0)
-    sent(s0, r0, 9)
+    lax.fori_loop(0, frames // FB, join_frames, 0)
+    wgrad_ref[...] = w_ref[...]
+    ggrad_ref[...] = g_ref[...] * grad_scale
+    kgrad_ref[...] = k_ref[...] * grad_scale
 
 
 def per_device(feats, cotan, lang, w_out, gain, kernel):
@@ -465,11 +518,6 @@
     taps = kernel.shape[1]
     total = owners * segs
     grad_scale = float(segs * frames) ** (-0.5)
-    group = LANES // segs
-    lane_owner = jnp.arange(LANES, dtype=jnp.int32) // segs
-    here = lane_owner == lax.axis_index("expert") % group
-    lang_row = jnp.where(here, jnp.tile(lang, group), 0).astype(F32)[None, :]
-
     shape = jax.ShapeDtypeStruct
     half = segs // 2
     whole = pltpu.VMEM((owners, frames // owners, segs, width), BF16)
@@ -480,22 +528,27 @@
     rows = pltpu.VMEM((frames // FB, FB, LANES), F32)
     dma = pltpu.SemaphoreType.DMA
     vmem = pl.BlockSpec(memory_space=pltpu.VMEM)
-    feat_grad, w_grad, gain_grad, tap_grad = pl.pallas_call(
+    home, w_grad, gain_grad, tap_grad = pl.pallas_call(
         functools.partial(module_kernel, owners, shards, grad_scale),
         out_shape=(
-            shape((segs, frames, width), BF16),
+            shape((2, owners, segs, width), BF16),
             shape(w_out.shape[1:], BF16),
             shape((1, width), F32),
             shape((taps, 1, width), F32),
         ),
-        in_specs=[vmem] * 6,
+        in_specs=[pl.BlockSpec(memory_space=pltpu.SMEM)] + [pl.BlockSpec(memory_space=pl.ANY)] * 3 + [vmem] * 2,
         out_specs=(vmem,) * 4,
         scratch_shapes=[
+            pltpu.VMEM(feats.shape, BF16),
+            pltpu.VMEM(feats.shape, BF16),
+            pltpu.VMEM(w_out.shape[1:], BF16),
             pltpu.VMEM((2, owners, 1, LANES), F32),
             *[whole] * 4,
             *[pltpu.VMEM((2,) + halves, BF16)] * 4,
             pltpu.VMEM((2, shards - 1) + halves, BF16),
-            pltpu.VMEM((2,) + halves, BF16),
+            pltpu.VMEM((2, 2, owners, half, width), BF16),
+            pltpu.VMEM((2, 2, owners, half, width), BF16),
+            pltpu.VMEM((2, owners, segs, width), BF16),
             pltpu.VMEM((total, total), BF16),
             pltpu.VMEM((total, total), BF16),
             f32_rows,
@@ -514,18 +567,31 @@
             rows,
             pltpu.VMEM((4, FB, LANES), F32),
             pltpu.VMEM((4, shards, FB, LANES), F32),
-            dma((10,)),
-            dma((10,)),
-            dma((2, 4)),
-            dma((2, 4)),
+            dma((13,)),
+            dma((13,)),
+            dma((2, 6)),
+            dma((2, 6)),
             dma((4, shards)),
             dma((4, shards)),
+            dma((3,)),
         ],
         compiler_params=pltpu.CompilerParams(
             collective_id=0, has_side_effects=True, vmem_limit_bytes=67043328
         ),
         name="module_backward",
-    )(lang_row, feats, cotan, w_out[0], gain, kernel[0])
+    )(lang, feats, cotan, w_out[0], gain, kernel[0])
+    feat_grad, w_grad, gain_grad, tap_grad = pl.pallas_call(
+        functools.partial(deliver_kernel, grad_scale),
+        out_shape=(
+            shape((segs, frames, width), BF16),
+            shape(w_out.shape[1:], BF16),
+            shape((1, width), F32),
+            shape((taps, 1, width), F32),
+        ),
+        in_specs=[vmem] * 4,
+        out_specs=(vmem,) * 4,
+        name="deliver",
+    )(home, w_grad, gain_grad, tap_grad)
     return feat_grad, w_grad[None], gain_grad, jnp.swapaxes(tap_grad, 0, 1)
 
 

time: 260 us -> 244 us (0.938)
  Pallas kernels: 253 us -> 243 us
  local copies, waits for them, and re-layouts: 5.8 us -> 0 us
    pallas_call x1, Pallas kernels: 253 us -> 239 us  [per_device(): pl.pallas_call(functools.partial(module_kernel, owners, shards, grad_scal...]
    unnamed x10 -> x0, local copies, waits for them, and re-layouts: 5.06 us -> none
    pallas_call x0 -> x1, Pallas kernels: none -> 4.12 us  [per_device(): pl.pallas_call(functools.partial(deliver_kernel, grad_scale), out_shape=(...]
where the time goes in v4:
time: 244 us; the launch traced here: 243 us
  Pallas kernels  243 us (100%)
    pallas_call x1, Pallas kernels, per_device(): pl.pallas_call(functools.partial(module_kernel, owners, shards, grad_scal...  239 us

profile of v4, /device:TPU:1, one launch (start us, length us, event | category | flops | bytes accessed | tf_op | source)
XLA Modules:
  0.0 243.3 jit_solution(4165171972071712369)
XLA Ops:
  0.6 238.6 %module_backward.1 = (bf16[2,64,16,384]{3,2,1,0:T(8,128)(2,1)}, bf16[384,1536]{1,0:T(8,128)(2,1)}, f32[1,384]{1,0:T(1,128)}, f32[31,1,384]{2,1,0:T(1,128)}) custom-call(s32[16]{0:T(128)} %lang_ref.1, bf16[16,128,384]{2,1,0:T(8,128)(2,1)} %x_ref.1, bf16[16,128,384]{2,1,0:T(8,128)(2,1)} %dy_ref.1, bf16[384,1536]{1,0:T(8,128)(2,1)} %bitcast.4, ...), custom_call_target="tpu_custom_call" | custom-call | tf_op jit(solution)/shard_map/module_backward/pallas_call | solution.py:531
  239.2 4.1 %deliver.1 = (bf16[16,128,384]{2,1,0:T(8,128)(2,1)}, bf16[384,1536]{1,0:T(8,128)(2,1)}, f32[1,384]{1,0:T(1,128)}, f32[31,1,384]{2,1,0:T(1,128)}) custom-call(bf16[2,64,16,384]{3,2,1,0:T(8,128)(2,1)} %get-tuple-element.12.home_ref, bf16[384,1536]{1,0:T(8,128)(2,1)} %get-tuple-element.13.w_ref, f32[1,384]{1,0:T(1,128)} %get-tuple-element.14.g_ref, ...), custom_call_target="tpu_custom_call" | custom-call | tf_op jit(solution)/shard_map/deliver/pallas_call | solution.py:583

commit v5 on v4

--- a/solution.py
+++ b/solution.py
@@ -46,7 +46,7 @@
     lang_ref, x_ref, dy_ref, w_ref, gain_ref, taps_ref,
     home_ref, wgrad_ref, ggrad_ref, kgrad_ref,
     x_vmem, dy_vmem, w_vmem, langs, s0, s1, r0, r1, p_dy, p_x, own_dy, own_x, ring, ret, back, home, pick, pick_t,
-    normed, conv, hidden, hid, gpad, spad, tapb, kacc, gacc, sum_a, sum_b, scale_c, rows_a, rows_b, mom, parts,
+    normed, slope, hidden, hid, gpad, spad, tapb, kacc, gacc, sum_a, sum_b, scale_c, rows_a, rows_b, mom, parts,
     send, recv, ring_send, ring_recv, ex_send, ex_recv, load,
 ):
     all_segs, frames, width = x_ref.shape
@@ -140,8 +140,10 @@
     for k in range(taps):
         tapb[k] = jnp.broadcast_to(taps_ref[k : k + 1, :].astype(F32), (segs, width))
     for pad in (gpad, spad):
-        pad[:half] = jnp.zeros((half, segs, LANES), F32)
-        pad[half + frames :] = jnp.zeros((pad.shape[0] - half - frames, segs, LANES), F32)
+        for h in range(2):
+            for c in range(chunks):
+                pad[h, c, :half] = jnp.zeros((half, segs, LANES), F32)
+                pad[h, c, half + frames :] = jnp.zeros((pad.shape[2] - half - frames, segs, LANES), F32)
     kacc[...] = jnp.zeros_like(kacc)
     gacc[...] = jnp.zeros_like(gacc)
 
@@ -344,18 +346,20 @@
 
             def fill(i, c):
                 at = pl.ds(i * FB, FB)
-                spad[pl.ds(i * FB + half, FB)] = normed[at, :, lanes] * gain[None]
+                spad[h, lb, pl.ds(i * FB + half, FB)] = normed[at, :, lanes] * gain[None]
                 return c
 
             lax.fori_loop(0, blocks, fill, 0)
 
             def step(i, c):
                 t = i * STEP
-                acc = tapb[0, :, lanes][None] * spad[pl.ds(t, STEP)]
+                acc = tapb[0, :, lanes][None] * spad[h, lb, pl.ds(t, STEP)]
                 for k in range(1, taps):
-                    acc = acc + tapb[k, :, lanes][None] * spad[pl.ds(t + k, STEP)]
-                conv[pl.ds(t, STEP), :, lanes] = acc
-                hidden[h, pl.ds(t, STEP), :, lanes] = (acc / (1.0 + jnp.exp(-acc))).astype(BF16)
+                    acc = acc + tapb[k, :, lanes][None] * spad[h, lb, pl.ds(t + k, STEP)]
+                gate = 1.0 / (1.0 + jnp.exp(-acc))
+                out = acc * gate
+                slope[pl.ds(t, STEP), :, lanes] = gate + out * (1.0 - gate)
+                hidden[h, pl.ds(t, STEP), :, lanes] = out.astype(BF16)
                 return c
 
             lax.fori_loop(0, frames // STEP, step, 0)
@@ -375,10 +379,7 @@
 
             def fill(i, c):
                 at = pl.ds(i * STEP, STEP)
-                a = conv[at, :, lanes]
-                s = 1.0 / (1.0 + jnp.exp(-a))
-                gpad[pl.ds(i * STEP + half, STEP)] = hid[at, :, lanes] * s * (1.0 + a * (1.0 - s))
-                spad[pl.ds(i * STEP + half, STEP)] = normed[at, :, lanes] * gain[None]
+                gpad[h, lb, pl.ds(i * STEP + half, STEP)] = hid[at, :, lanes] * slope[at, :, lanes]
                 return c
 
             lax.fori_loop(0, frames // STEP, fill, 0)
@@ -386,9 +387,9 @@
             def transposed(i, gain_sum):
                 t = i * STEP
                 at = pl.ds(t, STEP)
-                acc = tapb[0, :, lanes][None] * gpad[pl.ds(t + taps - 1, STEP)]
+                acc = tapb[0, :, lanes][None] * gpad[h, lb, pl.ds(t + taps - 1, STEP)]
                 for k in range(1, taps):
-                    acc = acc + tapb[k, :, lanes][None] * gpad[pl.ds(t + taps - 1 - k, STEP)]
+                    acc = acc + tapb[k, :, lanes][None] * gpad[h, lb, pl.ds(t + taps - 1 - k, STEP)]
                 hid[at, :, lanes] = acc
                 cross = acc * normed[at, :, lanes]
                 sum_a[at] = sum_a[at] + acc * gain[None]
@@ -398,14 +399,6 @@
             zero = jnp.zeros((segs, LANES), F32)
             gacc[:, lanes] = gacc[:, lanes] + lax.fori_loop(0, frames // STEP, transposed, zero)
 
-            def tap_sums(i, c):
-                t = i * STEP
-                g = gpad[pl.ds(t + half, STEP)]
-                for k in range(taps):
-                    kacc[k, :, lanes] = kacc[k, :, lanes] + jnp.sum(g * spad[pl.ds(t + k, STEP)], axis=0)
-                return c
-
-            lax.fori_loop(0, frames // STEP, tap_sums, 0)
             return carry
 
         lax.fori_loop(0, chunks, backward, 0)
@@ -458,7 +451,23 @@
     stage(0, lambda: start_ring(1), lambda: go_on_ring(1))
     stage(1, lambda: None, lambda: None)
 
+    def tap_grads(lb, carry):
+        lanes = pl.ds(pl.multiple_of(lb * LANES, LANES), LANES)
+        for h in range(2):
+
+            def tap_sums(i, c):
+                t = i * STEP
+                g = gpad[h, lb, pl.ds(t + half, STEP)]
+                for k in range(taps):
+                    term = jnp.sum(g * spad[h, lb, pl.ds(t + k, STEP)], axis=0)
+                    kacc[k, :, lanes] = kacc[k, :, lanes] + term
+                return c
+
+            lax.fori_loop(0, frames // STEP, tap_sums, 0)
+        return carry
+
     def weights():
+        lax.fori_loop(0, chunks, tap_grads, 0)
         for k in range(taps):
             kgrad_ref[k] = jnp.sum(kacc[k], axis=0, keepdims=True)
         ggrad_ref[...] = jnp.sum(gacc[...], axis=0, keepdims=True)
@@ -524,7 +533,7 @@
     halves = (owners, frames // owners, half, width)
     f32_rows = pltpu.VMEM((frames, half, width), F32)
     columns = pltpu.VMEM((frames, half, LANES), F32)
-    padded = pltpu.VMEM((frames + 32, half, LANES), F32)
+    padded = pltpu.VMEM((2, width // LANES, frames + 32, half, LANES), F32)
     rows = pltpu.VMEM((frames // FB, FB, LANES), F32)
     dma = pltpu.SemaphoreType.DMA
     vmem = pl.BlockSpec(memory_space=pltpu.VMEM)

time: 244 us -> 238 us (0.975)
  Pallas kernels: 243 us -> 237 us
    pallas_call x1, Pallas kernels: 239 us -> 233 us  [per_device(): pl.pallas_call(functools.partial(module_kernel, owners, shards, grad_scal...]
where the time goes in v5:
time: 238 us
  Pallas kernels  237 us (100%)
    pallas_call x1, Pallas kernels, per_device(): pl.pallas_call(functools.partial(module_kernel, owners, shards, grad_scal...  233 us

profile of v5, /device:TPU:1, one launch (start us, length us, event | category | flops | bytes accessed | tf_op | source)
XLA Modules:
  0.0 237.5 jit_solution(7999296263293561007)
XLA Ops:
  0.6 232.8 %module_backward.1 = (bf16[2,64,16,384]{3,2,1,0:T(8,128)(2,1)}, bf16[384,1536]{1,0:T(8,128)(2,1)}, f32[1,384]{1,0:T(1,128)}, f32[31,1,384]{2,1,0:T(1,128)}) custom-call(s32[16]{0:T(128)} %lang_ref.1, bf16[16,128,384]{2,1,0:T(8,128)(2,1)} %x_ref.1, bf16[16,128,384]{2,1,0:T(8,128)(2,1)} %dy_ref.1, bf16[384,1536]{1,0:T(8,128)(2,1)} %bitcast.4, ...), custom_call_target="tpu_custom_call" | custom-call | tf_op jit(solution)/shard_map/module_backward/pallas_call | solution.py:540
  233.4 4.1 %deliver.1 = (bf16[16,128,384]{2,1,0:T(8,128)(2,1)}, bf16[384,1536]{1,0:T(8,128)(2,1)}, f32[1,384]{1,0:T(1,128)}, f32[31,1,384]{2,1,0:T(1,128)}) custom-call(bf16[2,64,16,384]{3,2,1,0:T(8,128)(2,1)} %get-tuple-element.12.home_ref, bf16[384,1536]{1,0:T(8,128)(2,1)} %get-tuple-element.13.w_ref, f32[1,384]{1,0:T(1,128)} %get-tuple-element.14.g_ref, ...), custom_call_target="tpu_custom_call" | custom-call | tf_op jit(solution)/shard_map/deliver/pallas_call | solution.py:592

commit v6 on v5

--- a/solution.py
+++ b/solution.py
@@ -47,7 +47,7 @@
     home_ref, wgrad_ref, ggrad_ref, kgrad_ref,
     x_vmem, dy_vmem, w_vmem, langs, s0, s1, r0, r1, p_dy, p_x, own_dy, own_x, ring, ret, back, home, pick, pick_t,
     normed, slope, hidden, hid, gpad, spad, tapb, kacc, gacc, sum_a, sum_b, scale_c, rows_a, rows_b, mom, parts,
-    send, recv, ring_send, ring_recv, ex_send, ex_recv, load,
+    send, recv, ring_send, ring_recv, ex_send, ex_recv, load, w_block,
 ):
     all_segs, frames, width = x_ref.shape
     segs = own_x.shape[3]
@@ -88,21 +88,48 @@
 
         lax.fori_loop(0, blocks, block, 0)
 
-    def scatter(src, dst, i):
-        def one(p):
-            pltpu.make_async_remote_copy(
-                src_ref=src.at[p], dst_ref=dst.at[me], send_sem=send.at[i], recv_sem=recv.at[i],
-                device_id={"expert": p}, device_id_type=MESH,
-            ).start()
-
+    def pair_of(p):
+        return lax.rem(p, 2) * (owners // 2) + lax.div(p, 2)
+
+    def same(p):
+        return p
+
+    def send_block(src, dst, i, p, src_at, dst_at):
+        pltpu.make_async_remote_copy(
+            src_ref=src.at[src_at(p)], dst_ref=dst.at[dst_at(me)], send_sem=send.at[i], recv_sem=recv.at[i],
+            device_id={"expert": p}, device_id_type=MESH,
+        ).start()
+
+    def keep_block(src, dst, i, src_at, dst_at):
+        pltpu.make_async_copy(src.at[src_at(me)], dst.at[dst_at(me)], recv.at[i]).start()
+
+    def scatter(src, dst, i, src_at, dst_at):
         def both(d, carry):
-            one(lax.rem(me + d, owners))
-            one(lax.rem(me + owners - d, owners))
+            send_block(src, dst, i, lax.rem(me + d, owners), src_at, dst_at)
+            send_block(src, dst, i, lax.rem(me + owners - d, owners), src_at, dst_at)
             return carry
 
         lax.fori_loop(1, owners // 2, both, 0)
-        one(lax.rem(me + owners // 2, owners))
-        pltpu.make_async_copy(src.at[me], dst.at[me], recv.at[i]).start()
+        send_block(src, dst, i, lax.rem(me + owners // 2, owners), src_at, dst_at)
+        keep_block(src, dst, i, src_at, dst_at)
+
+    def scatter_half(src, dst, i, c):
+        count = owners // 2
+        mine = lax.div(me, 2)
+
+        def one(d, carry):
+            send_block(src, dst, i, lax.rem(mine + d, count) * 2 + c, pair_of, same)
+            return carry
+
+        lax.fori_loop(1, count, one, 0)
+
+        @pl.when(lax.rem(me, 2) == c)
+        def _():
+            keep_block(src, dst, i, pair_of, same)
+
+        @pl.when(lax.rem(me, 2) != c)
+        def _():
+            send_block(src, dst, i, mine * 2 + c, pair_of, same)
 
     def arrived(src, dst, i):
         pltpu.make_async_copy(src, dst, recv.at[i]).wait()
@@ -131,11 +158,11 @@
 
     lax.fori_loop(0, owners, spread_langs, 0)
     pl.semaphore_wait(barrier, owners - 1 + shards - 1)
-    scatter(langs_own, langs_all, 0)
-    scatter(s0, r0, 1)
+    scatter(langs_own, langs_all, 0, same, same)
+    scatter(s0, r0, 1, pair_of, same)
     loads[1].wait()
     split_frames(x_vmem, s1)
-    scatter(s1, r1, 2)
+    scatter(s1, r1, 2, pair_of, same)
 
     for k in range(taps):
         tapb[k] = jnp.broadcast_to(taps_ref[k : k + 1, :].astype(F32), (segs, width))
@@ -204,14 +231,14 @@
 
     arrived(s0, r0, 1)
     permute_out(0, r0, p_dy.at[0])
-    scatter(p_dy.at[0], own_dy.at[0], 3)
+    scatter(p_dy.at[0], own_dy.at[0], 3, same, pair_of)
     permute_out(1, r0, p_dy.at[1])
     arrived(s1, r1, 2)
     permute_out(0, r1, p_x.at[0])
-    scatter(p_x.at[0], own_x.at[0], 4)
-    scatter(p_dy.at[1], own_dy.at[1], 5)
+    scatter(p_x.at[0], own_x.at[0], 4, same, pair_of)
+    scatter(p_dy.at[1], own_dy.at[1], 5, same, pair_of)
     permute_out(1, r1, p_x.at[1])
-    scatter(p_x.at[1], own_x.at[1], 6)
+    scatter(p_x.at[1], own_x.at[1], 6, same, pair_of)
 
     def ring_copy(h, src, dst, i, d):
         return pltpu.make_async_remote_copy(
@@ -263,16 +290,16 @@
     def gathered(i):
         return [mom[i]] + [parts[i, d] for d in range(1, shards)]
 
-    def pack():
-        packed = rows_a[0]
-        for b in range(1, blocks):
-            packed = packed + pltpu.roll(rows_a[b], 2 * segs * b, 1)
+    def pack(first, last):
+        packed = rows_a[first]
+        for b in range(first + 1, last):
+            packed = packed + pltpu.roll(rows_a[b], 2 * segs * (b - first), 1)
         return packed
 
-    def unpack(packed, dst):
-        dst[0] = packed
-        for b in range(1, blocks):
-            dst[b] = pltpu.roll(packed, LANES - 2 * segs * b, 1)
+    def unpack(packed, dst, first, last):
+        dst[first] = packed
+        for b in range(first + 1, last):
+            dst[b] = pltpu.roll(packed, LANES - 2 * segs * (b - first), 1)
 
     def column(d):
         return pl.ds(pl.multiple_of(peer_x[d] * width, LANES), width)
@@ -296,8 +323,8 @@
             return carry
 
         lax.fori_loop(0, blocks, moments, 0)
-        mom[2 * h] = pack()
-        copies = exchange(2 * h)
+        mom[3 * h] = pack(0, blocks)
+        copies = exchange(3 * h)
         for copy in rings[h][:4]:
             copy.wait_recv()
         rings[h][4].start()
@@ -325,9 +352,9 @@
         lax.fori_loop(0, blocks // 2, hid_near, 0)
         for copy in copies:
             copy.wait()
-        mean_row, scale_row = mean_and_scale(gathered(2 * h), width, segs)
-        unpack(mean_row, rows_a)
-        unpack(scale_row, rows_b)
+        mean_row, scale_row = mean_and_scale(gathered(3 * h), width, segs)
+        unpack(mean_row, rows_a, 0, blocks)
+        unpack(scale_row, rows_b, 0, blocks)
 
         def normalize(b, carry):
             at = pl.ds(b * FB, FB)
@@ -373,16 +400,21 @@
         sum_a[...] = jnp.zeros_like(sum_a)
         sum_b[...] = jnp.zeros_like(sum_b)
 
-        def backward(lb, carry):
+        def slopes(lb, carry):
             lanes = pl.ds(pl.multiple_of(lb * LANES, LANES), LANES)
-            gain = gain_ref[:, lanes].astype(F32)
 
             def fill(i, c):
                 at = pl.ds(i * STEP, STEP)
                 gpad[h, lb, pl.ds(i * STEP + half, STEP)] = hid[at, :, lanes] * slope[at, :, lanes]
                 return c
 
-            lax.fori_loop(0, frames // STEP, fill, 0)
+            return lax.fori_loop(0, frames // STEP, fill, carry)
+
+        lax.fori_loop(0, chunks, slopes, 0)
+
+        def backward(first, last, lb, carry):
+            lanes = pl.ds(pl.multiple_of(lb * LANES, LANES), LANES)
+            gain = gain_ref[:, lanes].astype(F32)
 
             def transposed(i, gain_sum):
                 t = i * STEP
@@ -397,11 +429,9 @@
                 return gain_sum + jnp.sum(cross, axis=0)
 
             zero = jnp.zeros((segs, LANES), F32)
-            gacc[:, lanes] = gacc[:, lanes] + lax.fori_loop(0, frames // STEP, transposed, zero)
-
-            return carry
-
-        lax.fori_loop(0, chunks, backward, 0)
+            gacc[:, lanes] = gacc[:, lanes] + lax.fori_loop(first, last, transposed, zero)
+
+            return carry
 
         def sum_rows(b, carry):
             at = pl.ds(b * FB, FB)
@@ -409,11 +439,6 @@
             second = jnp.sum(sum_b[at], axis=2, keepdims=True)
             rows_a[b] = to_row(first, second, segs)
             return carry
-
-        lax.fori_loop(0, blocks, sum_rows, 0)
-        mom[2 * h + 1] = pack()
-        copies = exchange(2 * h + 1)
-        after()
 
         def prepare(b, carry):
             at = pl.ds(b * FB, FB)
@@ -422,13 +447,6 @@
             hid[at] = grads + scale * (hid[at] * gain_ref[...].astype(F32)[None])
             normed[at] = scale * normed[at]
             return carry
-
-        lax.fori_loop(0, blocks, prepare, 0)
-        for copy in copies:
-            copy.wait()
-        row = sum(gathered(2 * h + 1)) * (1.0 / (shards * width))
-        unpack(row, rows_a)
-        unpack(pltpu.roll(row, LANES - segs, 1), rows_b)
 
         def finish(b, carry):
             at = pl.ds(b * FB, FB)
@@ -441,9 +459,25 @@
                 ret[h, j, pl.ds(b * (FB // 2), FB // 2)] = out[:, j]
             return carry
 
-        lax.fori_loop(0, blocks, finish, 0)
-        for j in range(2):
-            scatter(ret.at[h, j], back.at[h, j], 7 + 2 * h + j)
+        spans = [(0, blocks // 2), (blocks // 2, blocks)]
+        steps = FB // STEP
+        copies = []
+        for c, (first, last) in enumerate(spans):
+            lax.fori_loop(0, chunks, functools.partial(backward, first * steps, last * steps), 0)
+            lax.fori_loop(first, last, sum_rows, 0)
+            mom[3 * h + 1 + c] = pack(first, last)
+            copies.append(exchange(3 * h + 1 + c))
+        after()
+        for c, (first, last) in enumerate(spans):
+            lax.fori_loop(first, last, prepare, 0)
+            for copy in copies[c]:
+                copy.wait()
+            row = sum(gathered(3 * h + 1 + c)) * (1.0 / (shards * width))
+            unpack(row, rows_a, first, last)
+            unpack(pltpu.roll(row, LANES - segs, 1), rows_b, first, last)
+            lax.fori_loop(first, last, finish, 0)
+            for j in range(2):
+                scatter_half(ret.at[h, j], back.at[h, j], 7 + 2 * h + j, c)
 
     loads[2].wait()
     start_ring(0)
@@ -481,15 +515,17 @@
                     (((0,), (0,)), ((), ())), preferred_element_type=F32,
                 )
                 block = term if block is None else block + term
-            wgrad_ref[:, column(d)] = (block * grad_scale).astype(BF16)
+            w_block[:, column(d)] = (block * grad_scale).astype(BF16)
 
     weights()
+    w_store = pltpu.make_async_copy(w_block, wgrad_ref, load.at[3])
+    w_store.start()
     sent(s0, r0, 1)
     for j in range(2):
         for h in range(2):
             arrived(ret.at[h, j], back.at[h, j], 7 + 2 * h + j)
         permute_home(j, home.at[j])
-        scatter(home.at[j], home_ref.at[j], 11 + j)
+        scatter(home.at[j], home_ref.at[j], 11 + j, same, pair_of)
     sent(langs_own, langs_all, 0)
     sent(s1, r1, 2)
     for h in range(2):
@@ -499,6 +535,7 @@
             sent(ret.at[h, j], back.at[h, j], 7 + 2 * h + j)
         for copy in rings[h]:
             copy.wait_send()
+    w_store.wait()
     for j in range(2):
         arrived(home.at[j], home_ref.at[j], 11 + j)
         sent(home.at[j], home_ref.at[j], 11 + j)
@@ -546,7 +583,7 @@
             shape((taps, 1, width), F32),
         ),
         in_specs=[pl.BlockSpec(memory_space=pltpu.SMEM)] + [pl.BlockSpec(memory_space=pl.ANY)] * 3 + [vmem] * 2,
-        out_specs=(vmem,) * 4,
+        out_specs=(pl.BlockSpec(memory_space=pl.ANY),) * 2 + (vmem,) * 2,
         scratch_shapes=[
             pltpu.VMEM(feats.shape, BF16),
             pltpu.VMEM(feats.shape, BF16),
@@ -574,15 +611,16 @@
             columns,
             rows,
             rows,
-            pltpu.VMEM((4, FB, LANES), F32),
-            pltpu.VMEM((4, shards, FB, LANES), F32),
+            pltpu.VMEM((6, FB, LANES), F32),
+            pltpu.VMEM((6, shards, FB, LANES), F32),
             dma((13,)),
             dma((13,)),
             dma((2, 6)),
             dma((2, 6)),
-            dma((4, shards)),
-            dma((4, shards)),
-            dma((3,)),
+            dma((6, shards)),
+            dma((6, shards)),
+            dma((4,)),
+            pltpu.VMEM(w_out.shape[1:], BF16),
         ],
         compiler_params=pltpu.CompilerParams(
             collective_id=0, has_side_effects=True, vmem_limit_bytes=67043328

time: 238 us -> 235 us (0.987)
  no operation moved by 1% of the time
where the time goes in v6:
time: 235 us
  Pallas kernels  235 us (100%)
    pallas_call x1, Pallas kernels, per_device(): pl.pallas_call(functools.partial(module_kernel, owners, shards, grad_scal...  230 us

profile of v6, /device:TPU:1, one launch (start us, length us, event | category | flops | bytes accessed | tf_op | source)
XLA Modules:
  0.0 235.2 jit_solution(6170484815856096211)
XLA Ops:
  0.6 230.4 %module_backward.1 = (bf16[2,64,16,384]{3,2,1,0:T(8,128)(2,1)}, bf16[384,1536]{1,0:T(8,128)(2,1)}, f32[1,384]{1,0:T(1,128)}, f32[31,1,384]{2,1,0:T(1,128)}) custom-call(s32[16]{0:T(128)} %lang_ref.1, bf16[16,128,384]{2,1,0:T(8,128)(2,1)} %x_ref.1, bf16[16,128,384]{2,1,0:T(8,128)(2,1)} %dy_ref.1, bf16[384,1536]{1,0:T(8,128)(2,1)} %bitcast.4, ...), custom_call_target="tpu_custom_call" | custom-call | tf_op jit(solution)/shard_map/module_backward/pallas_call | solution.py:577
  231.0 4.1 %deliver.1 = (bf16[16,128,384]{2,1,0:T(8,128)(2,1)}, bf16[384,1536]{1,0:T(8,128)(2,1)}, f32[1,384]{1,0:T(1,128)}, f32[31,1,384]{2,1,0:T(1,128)}) custom-call(bf16[2,64,16,384]{3,2,1,0:T(8,128)(2,1)} %get-tuple-element.12.home_ref, bf16[384,1536]{1,0:T(8,128)(2,1)} %get-tuple-element.13.w_ref, f32[1,384]{1,0:T(1,128)} %get-tuple-element.14.g_ref, ...), custom_call_target="tpu_custom_call" | custom-call | tf_op jit(solution)/shard_map/deliver/pallas_call | solution.py:630

commit v7 on v6

--- a/solution.py
+++ b/solution.py
@@ -541,20 +541,52 @@
         sent(home.at[j], home_ref.at[j], 11 + j)
 
 
-def deliver_kernel(grad_scale, home_ref, w_ref, g_ref, k_ref, feat_ref, wgrad_ref, ggrad_ref, kgrad_ref):
-    segs, frames, width = feat_ref.shape
+def deliver_kernel(
+    grad_scale, home_ref, w_ref, g_ref, k_ref, feat_ref, wgrad_ref, ggrad_ref, kgrad_ref,
+    home, feat, w_block, load, store,
+):
+    segs, frames, width = feat.shape
+    parts = 4
+    pairs = frames // 2 // parts
+    loads = [
+        pltpu.make_async_copy(
+            home_ref.at[:, p * pairs : (p + 1) * pairs], home.at[:, p * pairs : (p + 1) * pairs], load.at[p]
+        )
+        for p in range(parts)
+    ]
+    loads.append(pltpu.make_async_copy(w_ref, w_block, load.at[parts]))
+    stores = [
+        pltpu.make_async_copy(
+            feat.at[:, 2 * p * pairs : 2 * (p + 1) * pairs],
+            feat_ref.at[:, 2 * p * pairs : 2 * (p + 1) * pairs],
+            store.at[p],
+        )
+        for p in range(parts)
+    ]
+    stores.append(pltpu.make_async_copy(w_block, wgrad_ref, store.at[parts]))
+    for copy in loads:
+        copy.start()
 
     def join_frames(b, carry):
         at = pl.ds(b * (FB // 2), FB // 2)
-        rows = jnp.stack([home_ref[0, at].astype(F32), home_ref[1, at].astype(F32)], axis=1)
+        rows = jnp.stack([home[0, at].astype(F32), home[1, at].astype(F32)], axis=1)
         rows = rows.reshape(FB, segs, width)
-        feat_ref[:, pl.ds(pl.multiple_of(b * FB, FB), FB), :] = jnp.swapaxes(rows, 0, 1).astype(BF16)
+        feat[:, pl.ds(pl.multiple_of(b * FB, FB), FB), :] = jnp.swapaxes(rows, 0, 1).astype(BF16)
         return carry
 
-    lax.fori_loop(0, frames // FB, join_frames, 0)
-    wgrad_ref[...] = w_ref[...]
+    each = 2 * pairs // FB
+    for p in range(parts):
+        loads[p].wait()
+        lax.fori_loop(p * each, (p + 1) * each, join_frames, 0)
+        if p > 0:
+            stores[p - 1].start()
+    loads[parts].wait()
+    stores[parts].start()
     ggrad_ref[...] = g_ref[...] * grad_scale
     kgrad_ref[...] = k_ref[...] * grad_scale
+    stores[parts - 1].start()
+    for copy in stores:
+        copy.wait()
 
 
 def per_device(feats, cotan, lang, w_out, gain, kernel):
@@ -635,8 +667,15 @@
             shape((1, width), F32),
             shape((taps, 1, width), F32),
         ),
-        in_specs=[vmem] * 4,
-        out_specs=(vmem,) * 4,
+        in_specs=[pl.BlockSpec(memory_space=pl.ANY)] * 2 + [vmem] * 2,
+        out_specs=(pl.BlockSpec(memory_space=pl.ANY),) * 2 + (vmem,) * 2,
+        scratch_shapes=[
+            pltpu.VMEM((2, owners, segs, width), BF16),
+            pltpu.VMEM((segs, frames, width), BF16),
+            pltpu.VMEM(w_out.shape[1:], BF16),
+            dma((5,)),
+            dma((5,)),
+        ],
         name="deliver",
     )(home, w_grad, gain_grad, tap_grad)
     return feat_grad, w_grad[None], gain_grad, jnp.swapaxes(tap_grad, 0, 1)

time: 235 us -> 236 us (level)
  no operation moved by 1% of the time
where the time goes in v7:
time: 236 us
  Pallas kernels  235 us (100%)
    pallas_call x1, Pallas kernels, per_device(): pl.pallas_call(functools.partial(module_kernel, owners, shards, grad_scal...  230 us

profile of v7, /device:TPU:1, one launch (start us, length us, event | category | flops | bytes accessed | tf_op | source)
XLA Modules:
  0.0 235.7 jit_solution(18164452816617820424)
XLA Ops:
  0.6 230.4 %module_backward.1 = (bf16[2,64,16,384]{3,2,1,0:T(8,128)(2,1)}, bf16[384,1536]{1,0:T(8,128)(2,1)}, f32[1,384]{1,0:T(1,128)}, f32[31,1,384]{2,1,0:T(1,128)}) custom-call(s32[16]{0:T(128)} %lang_ref.1, bf16[16,128,384]{2,1,0:T(8,128)(2,1)} %x_ref.1, bf16[16,128,384]{2,1,0:T(8,128)(2,1)} %dy_ref.1, bf16[384,1536]{1,0:T(8,128)(2,1)} %bitcast.4, ...), custom_call_target="tpu_custom_call" | custom-call | tf_op jit(solution)/shard_map/module_backward/pallas_call | solution.py:609
  231.0 4.5 %deliver.1 = (bf16[16,128,384]{2,1,0:T(8,128)(2,1)}, bf16[384,1536]{1,0:T(8,128)(2,1)}, f32[1,384]{1,0:T(1,128)}, f32[31,1,384]{2,1,0:T(1,128)}) custom-call(bf16[2,64,16,384]{3,2,1,0:T(8,128)(2,1)} %get-tuple-element.12.home_ref, bf16[384,1536]{1,0:T(8,128)(2,1)} %get-tuple-element.13.w_ref, f32[1,384]{1,0:T(1,128)} %get-tuple-element.14.g_ref, ...), custom_call_target="tpu_custom_call" | custom-call | tf_op jit(solution)/shard_map/deliver/pallas_call | solution.py:662
